TPU v7x, 512 devices: a whole 4x4x16 slice. The times are simulated.
512 devices in a mesh: dp: 64 (over y, z), mp: 8 (over x, core).
Axes of the slice: x: 4, y: 4, z: 16, core: 2. Of those that a mesh axis runs over, the one named last changes fastest.
Arguments:
- x_in: bfloat16 [25600, 2048], P('dp'), may hold values from -6 to 6
- cotangent: bfloat16 [25600, 7168], P('dp', 'mp'), may hold values from -6 to 6
- w_gate: bfloat16 [2048, 7168], P('dp', 'mp'), may hold values from -0.125 to 0.125
- w_up: bfloat16 [2048, 7168], P('dp', 'mp'), may hold values from -0.125 to 0.125
- send_counts: int32 [64, 64], P('dp'), may hold values from 0 to 4, as said below
- recv_counts: int32 [64, 64], P('dp'), may hold values from 0 to 4, as said below
Outputs:
- grad_x: bfloat16 [25600, 2048], P('dp', 'mp')
- grad_gate: float32 [2048, 7168], P('dp', 'mp')
Inputs may be any that keep to these rules, and one draw needn't show every extreme that they name: `send_counts`: each entry is 0 to 4. A quarter of the indices only send and the rest only receive; one sending index sends 4 rows to every receiver, so its live rows reach 400. recv_counts is the transpose of send_counts.
All inputs are finite; a program needn't handle non-finite values.
Results may differ from a plain program's by a relative error of at most 0.014.
Values may be sent and summed in bfloat16 or wider, within the bound.
A program may use at most 64 MiB of HBM per device.

v0:
```python
import jax
import jax.numpy as jnp
from jax import lax
from jax.sharding import PartitionSpec as P

BAL = 208


def contract_last(left, right):
    return lax.dot_general(
        left, right, (((1,), (1,)), ((), ())), preferred_element_type=jnp.float32
    )


def swiglu_back(x_rows, cot_rows, gate_full, up_full, live_mask):
    gate_val = jnp.dot(x_rows, gate_full, preferred_element_type=jnp.float32)
    up_val = jnp.dot(x_rows, up_full, preferred_element_type=jnp.float32)
    sig = jax.nn.sigmoid(gate_val)
    cot_val = cot_rows.astype(jnp.float32)
    d_gate = jnp.where(
        live_mask[:, None], cot_val * up_val * sig * (1.0 + gate_val * (1.0 - sig)), 0.0
    ).astype(jnp.bfloat16)
    d_up = jnp.where(live_mask[:, None], cot_val * gate_val * sig, 0.0).astype(jnp.bfloat16)
    partial_value = contract_last(d_gate, gate_full) + contract_last(d_up, up_full)
    return (partial_value, d_gate)


def group_sum(partial_value):
    return lax.psum_scatter(
        partial_value.astype(jnp.bfloat16), "mp", scatter_dimension=1, tiled=True
    )


def on_device(x_in, cotangent, w_gate, w_up, send_counts, recv_counts):
    rows_cap = x_in.shape[0]
    width = x_in.shape[1]
    dev_count = lax.axis_size("dp")
    gate_full, up_full = (
        lax.all_gather(w_gate, "dp", axis=0, tiled=True),
        lax.all_gather(w_up, "dp", axis=0, tiled=True),
    )
    sent = send_counts[0]
    got = recv_counts[0]
    live_rows = BAL + jnp.sum(sent) - jnp.sum(got)
    live_mask = jnp.arange(rows_cap) < live_rows
    partial_value, d_gate = swiglu_back(x_in, cotangent, gate_full, up_full, live_mask)
    grad_x = group_sum(partial_value)
    block_rows = width // dev_count
    whole = lax.dot_general(
        x_in, d_gate, (((0,), (0,)), ((), ())), preferred_element_type=jnp.float32
    )
    pieces = lax.all_to_all(
        whole.reshape(dev_count, block_rows, whole.shape[1]),
        "dp",
        split_axis=0,
        concat_axis=0,
        tiled=True,
    )
    grad_gate = jnp.sum(pieces, axis=0)
    return (grad_x, grad_gate)


def solution(mesh):
    return jax.shard_map(
        on_device,
        mesh=mesh,
        in_specs=(
            P("dp", None),
            P("dp", "mp"),
            P("dp", "mp"),
            P("dp", "mp"),
            P("dp", None),
            P("dp", None),
        ),
        out_specs=(P("dp", "mp"), P("dp", "mp")),
        check_vma=False,
    )
```

profile of v0, /device:TPU:1, one launch (start us, length us, event | category | flops | bytes accessed | tf_op | source)
XLA Modules:
  0.0 644.2 jit_solution(2757115259836697737)
XLA Ops:
  7.2 0.0 copy-start
  7.2 0.0 all-gather.5.cloned.1.call-start
  7.2 0.7 all-gather.5.cloned.1.call-update
  7.9 0.0 all-gather.3.cloned.1.call-start
  8.0 0.7 all-gather.3.cloned.1.call-update
  8.7 1.3 reduce_sum.28
  10.0 1.3 reduce_sum.27
  12.6 0.0 copy-start.2
  12.6 139.8 %all-gather.5.cloned.1.call-done = bf16[2048,896]{1,0:T(8,128)(2,1)} async-done(((bf16[32,896]{1,0:T(8,128)(2,1)}), bf16[2048,896]{1,0:T(8,128)(2,1)}) %all-gather.5.cloned.1.call-update) | async-done | bytes 3670032 | tf_op jit(solution)/shard_map/all_gather | solution.py:39
  152.4 0.0 copy-done
  152.4 5.0 fusion.11
  157.5 137.7 %all-gather.3.cloned.1.call-done = bf16[2048,896]{1,0:T(8,128)(2,1)} async-done(((bf16[32,896]{1,0:T(8,128)(2,1)}), bf16[2048,896]{1,0:T(8,128)(2,1)}) %all-gather.3.cloned.1.call-update) | async-done | bytes 3670032 | tf_op jit(solution)/shard_map/all_gather | solution.py:40
  295.1 0.0 copy-done.2
  295.1 4.6 select_convert_fusion
  299.7 5.1 convolution_bitcast_fusion
  304.8 8.6 %copy.8 = f32[2048,896]{1,0:T(8,128)} copy(f32[2048,896]{0,1:T(8,128)} %convolution_bitcast_fusion) | data formatting | bytes 14680064 | tf_op jit(solution)/shard_map/dot_general | solution.py:49
  313.4 9.7 %all-to-all-start = ((f32[64,32,896]{2,1,0:T(8,128)}), f32[64,32,896]{2,1,0:T(8,128)}, u32[]{:S(2)}, u32[]{:S(2)}) async-start(f32[64,32,896]{2,1,0:T(8,128)} %bitcast.12), calls=%async_computation.1 | async-start | bytes 14680064 | tf_op jit(solution)/shard_map/all_to_all | solution.py:52
  323.1 0.0 reduce-scatter.2.cloned.1.call-start
  323.1 0.0 copy-start.1
  323.1 0.0 copy-start.3
  323.1 4.1 fusion.12
  327.2 0.0 copy-done.1
  327.2 0.0 copy-done.3
  327.2 3.1 add_convert_fusion
  330.4 0.0 reduce-scatter.2.cloned.1.call-update
  330.4 303.2 %all-to-all-done = f32[64,32,896]{2,1,0:T(8,128)} async-done(((f32[64,32,896]{2,1,0:T(8,128)}), f32[64,32,896]{2,1,0:T(8,128)}, u32[]{:S(2)}, u32[]{:S(2)}) %all-to-all-start) | async-done | bytes 7340064 | tf_op jit(solution)/shard_map/all_to_all | solution.py:52
  633.6 4.1 reduce_sum.29
  637.7 0.0 reduce-scatter.2.cloned.1.call-done
  (1 shorter events, 0.0 us)
Async XLA Ops:
  7.2 145.3 %copy-start = (bf16[400,2048]{1,0:T(8,128)(2,1)S(1)}, bf16[400,2048]{1,0:T(8,128)(2,1)}, u32[]{:S(2)}) copy-start(bf16[400,2048]{1,0:T(8,128)(2,1)} %param.6) | copy-start | bytes 4915204
  7.2 145.2 %all-gather.5.cloned.1.call-start = ((), (), s32[]{:S(2)}) async-start(), calls=%async_computation.3 | async-start | bytes 3727360 | tf_op jit(solution)/shard_map/all_gather | solution.py:39
  7.9 287.2 %all-gather.3.cloned.1.call-start = ((), (), s32[]{:S(2)}) async-start(), calls=%async_computation.2 | async-start | bytes 3727360 | tf_op jit(solution)/shard_map/all_gather | solution.py:40
  12.6 282.6 %copy-start.2 = (bf16[400,896]{1,0:T(8,128)(2,1)S(1)}, bf16[400,896]{1,0:T(8,128)(2,1)}, u32[]{:S(2)}) copy-start(bf16[400,896]{1,0:T(8,128)(2,1)} %param.7) | copy-start | bytes 2150404
  313.4 320.2 %all-to-all-start = ((f32[64,32,896]{2,1,0:T(8,128)}), f32[64,32,896]{2,1,0:T(8,128)}, u32[]{:S(2)}, u32[]{:S(2)}) async-start(f32[64,32,896]{2,1,0:T(8,128)} %bitcast.12), calls=%async_computation.1 | async-start | bytes 14680064 | tf_op jit(solution)/shard_map/all_to_all | solution.py:52
  323.1 314.6 %reduce-scatter.2.cloned.1.call-start = ((), (), s32[]{:S(2)}) async-start(), calls=%async_computation.4 | async-start | bytes 1843200 | tf_op jit(solution)/shard_map/reduce_scatter | solution.py:29
  323.1 4.1 copy-start.1
  323.1 4.1 copy-start.3
Sparse Core Ops, SparseCore 0:
  11.0 141.4 all-gather.4
  155.4 139.7 all-gather.2
  330.5 48.7 reduce-scatter.1
where the time goes:
time: 656 us; the launch traced here: 644 us
  waiting for transfers between devices  582 us (89%)
  matrix products  21.9 us (3%)
  between operations  15.1 us (2%)
  starting transfers between devices  9.77 us (1%)
  local copies, waits for them, and re-layouts  8.61 us (1%)
  other arithmetic  6.68 us (1%)
    all_to_all x1, waiting for transfers between devices, on_device(): lax.all_to_all(whole.reshape(dev_count, block_rows, whole.shape[1]), 'dp'...  303 us
    all_gather x1, waiting for transfers between devices, on_device(): lax.all_gather(w_gate, 'dp', axis=0, tiled=True)  140 us
    all_gather x1, waiting for transfers between devices, on_device(): lax.all_gather(w_up, 'dp', axis=0, tiled=True)  138 us
  transfers between devices with their start and end apart: 4, of which 3 were waited for; matrix products, arithmetic and copies ran while one was open for 3% of the time, Pallas kernels for 0%

commit v1 on v0

--- a/solution.py
+++ b/solution.py
@@ -49,14 +49,7 @@
     whole = lax.dot_general(
         x_in, d_gate, (((0,), (0,)), ((), ())), preferred_element_type=jnp.float32
     )
-    pieces = lax.all_to_all(
-        whole.reshape(dev_count, block_rows, whole.shape[1]),
-        "dp",
-        split_axis=0,
-        concat_axis=0,
-        tiled=True,
-    )
-    grad_gate = jnp.sum(pieces, axis=0)
+    grad_gate = lax.psum_scatter(whole.astype(jnp.bfloat16), "dp", scatter_dimension=0, tiled=True).astype(jnp.float32)
     return (grad_x, grad_gate)
 
 

time: 656 us -> 1060 us (1.62); the launches traced: 644 us -> 1060 us
  waiting for transfers between devices: 582 us -> 1010 us
    unnamed x3 -> x5, waiting for transfers between devices: 1.39 us -> 687 us
    all_to_all x1 -> x0, waiting for transfers between devices: 303 us -> none  [on_device(): lax.all_to_all(whole.reshape(dev_count, block_rows, whole.shape[1]), 'dp'...]
    reduce_scatter x1, waiting for transfers between devices: 0.01 us -> 48.8 us  [group_sum(): lax.psum_scatter(partial_value.astype(jnp.bfloat16), 'mp', scatter_dimens...]
  transfers between devices with their start and end apart: 4 -> 4, of which waited for: 3 -> 4; matrix products, arithmetic and copies ran while one was open for 3% -> 2% of each run, Pallas kernels for 0% -> 0%
where the time goes in v1:
time: 1060 us
  waiting for transfers between devices  1010 us (95%)
  matrix products  20.8 us (2%)
  between operations  15.1 us (1%)
    unnamed x5, waiting for transfers between devices  687 us
    all_gather x1, waiting for transfers between devices, on_device(): lax.all_gather(w_gate, 'dp', axis=0, tiled=True)  140 us
    all_gather x1, waiting for transfers between devices, on_device(): lax.all_gather(w_up, 'dp', axis=0, tiled=True)  138 us
    reduce_scatter x1, waiting for transfers between devices, group_sum(): lax.psum_scatter(partial_value.astype(jnp.bfloat16), 'mp', scatter_dimens...  48.8 us
  transfers between devices with their start and end apart: 4, of which 4 were waited for; matrix products, arithmetic and copies ran while one was open for 2% of the time, Pallas kernels for 0%

profile of v1, /device:TPU:1, one launch (start us, length us, event | category | flops | bytes accessed | tf_op | source)
XLA Modules:
  0.0 1059.7 jit_solution(8219626550588682840)
XLA Ops:
  7.2 0.0 copy-start
  7.2 0.0 all-gather.5.cloned.1.call-start
  7.2 0.7 all-gather.5.cloned.1.call-update
  7.9 0.0 all-gather.3.cloned.1.call-start
  8.0 0.7 all-gather.3.cloned.1.call-update
  8.7 0.0 reduce-scatter.7.cloned.1.call-start
  8.7 1.3 reduce_sum.19
  10.0 1.3 reduce_sum.18
  12.6 0.0 copy-start.2
  12.6 139.8 %all-gather.5.cloned.1.call-done = bf16[2048,896]{1,0:T(8,128)(2,1)} async-done(((bf16[32,896]{1,0:T(8,128)(2,1)}), bf16[2048,896]{1,0:T(8,128)(2,1)}) %all-gather.5.cloned.1.call-update) | async-done | bytes 3670032 | tf_op jit(solution)/shard_map/all_gather | solution.py:39
  152.4 0.0 copy-done
  152.4 5.0 fusion.11
  157.5 137.7 %all-gather.3.cloned.1.call-done = bf16[2048,896]{1,0:T(8,128)(2,1)} async-done(((bf16[32,896]{1,0:T(8,128)(2,1)}), bf16[2048,896]{1,0:T(8,128)(2,1)}) %all-gather.3.cloned.1.call-update) | async-done | bytes 3670032 | tf_op jit(solution)/shard_map/all_gather | solution.py:40
  295.1 0.0 copy-done.2
  295.1 4.6 select_convert_fusion
  299.7 4.0 convert_bitcast_fusion
  303.7 6.1 copy.10
  309.8 0.0 reduce-scatter.7.cloned.1.call-update
  309.9 0.0 reduce-scatter.5.cloned.1.call-start
  309.9 0.0 copy-start.1
  309.9 0.0 copy-start.3
  309.9 4.1 fusion.12
  314.0 0.0 copy-done.1
  314.0 0.0 copy-done.3
  314.0 3.1 add_convert_fusion
  317.2 0.0 reduce-scatter.5.cloned.1.call-update
  317.2 685.4 %reduce-scatter.7.cloned.1.call-done = bf16[32,896]{1,0:T(8,128)(2,1)} async-done(((bf16[2048,896]{1,0:T(8,128)(2,1)}), bf16[32,896]{1,0:T(8,128)(2,1)}) %reduce-scatter.7.cloned.1.call-update) | async-done | bytes 57360
  1002.6 1.0 copy.11
  1003.6 0.8 copy.9
  1004.4 48.8 %reduce-scatter.5.cloned.1.call-done = bf16[400,256]{1,0:T(8,128)(2,1)} async-done(((bf16[400,2048]{1,0:T(8,128)(2,1)}), bf16[400,256]{1,0:T(8,128)(2,1)}) %reduce-scatter.5.cloned.1.call-update) | async-done | bytes 204816 | tf_op jit(solution)/shard_map/reduce_scatter | solution.py:29
  (1 shorter events, 0.0 us)
Async XLA Ops:
  7.2 145.3 %copy-start = (bf16[400,2048]{1,0:T(8,128)(2,1)S(1)}, bf16[400,2048]{1,0:T(8,128)(2,1)}, u32[]{:S(2)}) copy-start(bf16[400,2048]{1,0:T(8,128)(2,1)} %param.6) | copy-start | bytes 4915204
  7.2 145.2 %all-gather.5.cloned.1.call-start = ((), (), s32[]{:S(2)}) async-start(), calls=%async_computation.3 | async-start | bytes 3727360 | tf_op jit(solution)/shard_map/all_gather | solution.py:39
  7.9 287.2 %all-gather.3.cloned.1.call-start = ((), (), s32[]{:S(2)}) async-start(), calls=%async_computation.2 | async-start | bytes 3727360 | tf_op jit(solution)/shard_map/all_gather | solution.py:40
  8.7 993.9 %reduce-scatter.7.cloned.1.call-start = ((), (), s32[]{:S(2)}) async-start(), calls=%async_computation.5 | async-start | bytes 3727360
  12.6 282.5 %copy-start.2 = (bf16[400,896]{1,0:T(8,128)(2,1)S(1)}, bf16[400,896]{1,0:T(8,128)(2,1)}, u32[]{:S(2)}) copy-start(bf16[400,896]{1,0:T(8,128)(2,1)} %param.7) | copy-start | bytes 2150404
  309.9 743.3 %reduce-scatter.5.cloned.1.call-start = ((), (), s32[]{:S(2)}) async-start(), calls=%async_computation.4 | async-start | bytes 1843200 | tf_op jit(solution)/shard_map/reduce_scatter | solution.py:29
  309.9 4.1 copy-start.1
  309.9 4.1 copy-start.3
Sparse Core Ops, SparseCore 0:
  11.0 141.4 all-gather.4
  155.4 139.7 all-gather.2
  310.0 692.5 reduce-scatter.6
  1006.1 46.9 reduce-scatter.4

commit v2 on v1

v2 whole, which is shorter than its diff:
```python
import functools

import jax
import jax.numpy as jnp
from jax import lax
from jax.experimental import pallas as pl
from jax.experimental.pallas import tpu as pltpu
from jax.sharding import PartitionSpec as P

BAL = 208
RING_Y = 4
MESH = pl.DeviceIdType.MESH
VMEM = pl.BlockSpec(memory_space=pltpu.VMEM)


def place(nz):
    me = lax.axis_index("dp")
    y, z = lax.div(me, nz), lax.rem(me, nz)

    def index(yo, zo):
        return lax.rem(y + yo + 2 * RING_Y, RING_Y) * nz + lax.rem(z + zo + 2 * nz, nz)

    return index


def greet(index):
    barrier = pltpu.get_barrier_semaphore()
    for yo, zo in ((0, 1), (0, -1), (1, 0), (-1, 0)):
        pl.semaphore_signal(
            barrier, inc=1, device_id={"dp": index(yo, zo)}, device_id_type=MESH
        )
    pl.semaphore_wait(barrier, 4)


def reach(nz, stream, way):
    forward = stream in ("a", 0)
    return nz // 2 if forward == (way == 0) else nz // 2 - 1


def gather_kernel(
    nz, cut, half_a, half_b, w_ref, out_ref, za_s, za_r, zb_s, zb_r, ya_s, ya_r, yb_s, yb_r, own
):
    index = place(nz)
    rows, cols = w_ref.shape
    top = nz // 2
    spans = {"a": (0, cut), "b": (cut, cols - cut)}
    halves = {
        "a": ((0, half_a), (half_a, cut - half_a)),
        "b": ((cut, half_b), (cut + half_b, cols - cut - half_b)),
    }

    def block(yo, zo, span):
        start = pl.multiple_of(index(yo, zo) * rows, rows)
        return out_ref.at[pl.ds(start, rows), pl.ds(span[0], span[1])]

    def copy(src, dst, target, s_sem, r_sem):
        return pltpu.make_async_remote_copy(
            src_ref=src, dst_ref=dst, send_sem=s_sem, recv_sem=r_sem,
            device_id={"dp": index(*target)}, device_id_type=MESH,
        )

    def origin(way, k):
        return -k if way == 0 else k

    def onward(way):
        return (0, 1) if way == 0 else (0, -1)

    def z_copy(stream, way, k, mine=False):
        span = spans["a"] if stream == "a" else spans["b"]
        yo = 0 if stream == "a" else stream
        dst = block(yo, origin(way, k - 1), span)
        src = w_ref.at[:, pl.ds(span[0], span[1])] if mine else dst
        sems = (za_s.at[way, k], za_r.at[way, k]) if stream == "a" else (
            zb_s.at[way, k, stream], zb_r.at[way, k, stream])
        return copy(src, dst, onward(way), *sems)

    def z_wait(stream, way, k):
        span = spans["a"] if stream == "a" else spans["b"]
        yo = 0 if stream == "a" else stream
        dst = block(yo, origin(way, k), span)
        sem = za_r.at[way, k] if stream == "a" else zb_r.at[way, k, stream]
        other = za_s.at[way, k] if stream == "a" else zb_s.at[way, k, stream]
        copy(dst, dst, onward(way), other, sem).wait_recv()

    def y_sems(kind, c, part):
        if kind == "a":
            return ya_s.at[c, part], ya_r.at[c, part]
        return yb_s.at[part], yb_r.at[part]

    def y_part(kind, part):
        return spans[kind] if part < 2 else halves[kind][part - 2]

    def y_copy(kind, zo, c, part, mine=False):
        span = y_part(kind, part)
        yo = 0 if part < 2 else (-1 if part == 2 else 1)
        dst = block(yo, zo, span)
        src = w_ref.at[:, pl.ds(span[0], span[1])] if mine else dst
        return copy(src, dst, (1, 0) if part % 2 == 0 else (-1, 0), *y_sems(kind, c, part))

    def y_wait(kind, zo, c, part):
        yo = (-1, 1, -2, 2)[part]
        dst = block(yo, zo, y_part(kind, part))
        copy(dst, dst, (1, 0), *y_sems(kind, c, part)).wait_recv()

    def cell(way, k):
        return 2 * k - 1 + way

    def y_pass(kind, zo, c):
        for part in (0, 1):
            y_wait(kind, zo, c, part)
            y_copy(kind, zo, c, part + 2).start()

    greet(index)
    keep = pltpu.make_async_copy(w_ref, out_ref.at[pl.ds(pl.multiple_of(index(0, 0) * rows, rows), rows), :], own)
    keep.start()
    for part in (0, 1):
        y_copy("b", 0, 0, part, True).start()
    for way in (0, 1):
        z_copy("a", way, 1, True).start()
        z_copy(0, way, 1, True).start()
    for part in (0, 1):
        y_copy("a", 0, 0, part, True).start()
    for part in (0, 1):
        y_wait("b", 0, 0, part)
        y_copy("b", 0, 0, part + 2).start()
        for way in (0, 1):
            z_copy(3 if part == 0 else 1, way, 1).start()

    def step(k, known, first=False):
        def arrives(stream, way):
            return not known or k <= reach(nz, stream, way)

        def goes_on(stream, way):
            return not known or k + 1 <= reach(nz, stream, way)

        for way in (0, 1):
            if arrives("a", way):
                z_wait("a", way, k)
                if goes_on("a", way):
                    z_copy("a", way, k + 1).start()
                for part in (0, 1):
                    y_copy("a", origin(way, k), cell(way, k), part).start()
        if first:
            for part in (2, 3):
                y_wait("b", 0, 0, part)
            for way in (0, 1):
                z_copy(2, way, 1).start()
        for stream in (0, 3, 1, 2):
            for way in (0, 1):
                if arrives(stream, way):
                    z_wait(stream, way, k)
                    if goes_on(stream, way):
                        z_copy(stream, way, k + 1).start()
        if first:
            y_pass("a", 0, 0)
        else:
            for way in (0, 1):
                y_pass("a", origin(way, k - 1), cell(way, k - 1))

    step(1, True, True)
    if top > 3:
        def body(k, carry):
            step(k, False)
            return carry

        lax.fori_loop(2, top - 1, body, 0)
    if top > 2:
        step(top - 1, True)
    step(top, True)
    y_pass("a", -top, cell(0, top))

    def drain_y(c, zo):
        for part in (2, 3):
            y_wait("a", zo, c, part)
        for part in range(4):
            y_copy("a", zo, c, part).wait_send()

    drain_y(0, 0)
    for part in range(4):
        y_copy("b", 0, 0, part).wait_send()

    def drain(k, known):
        for way in (0, 1):
            for stream in ("a", 0, 1, 2, 3):
                if not known or k <= reach(nz, stream, way):
                    z_copy(stream, way, k).wait_send()
            if not known or k <= reach(nz, "a", way):
                drain_y(cell(way, k), origin(way, k))

    def drain_body(k, carry):
        drain(k, False)
        return carry

    lax.fori_loop(1, top, drain_body, 0)
    drain(top, True)
    keep.wait()


def gather_rows(shard, ranks):
    rows, cols = shard.shape
    nz = ranks // RING_Y
    tiles = cols // 128
    cut = 128 * max(2, round(tiles * 0.633))
    half_a = 128 * ((cut // 128 + 1) // 2)
    half_b = 128 * (((cols - cut) // 128 + 1) // 2)
    dma = pltpu.SemaphoreType.DMA
    k = nz // 2 + 1
    return pl.pallas_call(
        functools.partial(gather_kernel, nz, cut, half_a, half_b),
        out_shape=jax.ShapeDtypeStruct((ranks * rows, cols), shard.dtype),
        in_specs=[VMEM],
        out_specs=pl.BlockSpec(memory_space=pl.ANY),
        scratch_shapes=[
            dma((2, k)), dma((2, k)), dma((2, k, 4)), dma((2, k, 4)),
            dma((nz, 4)), dma((nz, 4)), dma((4,)), dma((4,)), dma,
        ],
        compiler_params=pltpu.CompilerParams(collective_id=0, has_side_effects=True),
        name="gather_rows",
    )(shard)


def scatter_kernel(
    nz, cut, half_a, half_b, p_ref, out_ref,
    far, near, near_out, za_in, za_out, zb_in, zb_out, b_sum, b_far, b_near, b_near_out,
    far_s, far_r, near_s, near_r, za_s, za_r, zb_s, zb_r, bf_s, bf_r, bn_s, bn_r,
):
    index = place(nz)
    rows, cols = out_ref.shape
    top = nz // 2
    f32, bf16 = jnp.float32, jnp.bfloat16
    wide_b = cols - cut
    halves_a = ((0, half_a), (half_a, cut - half_a))
    halves_b = ((0, half_b), (half_b, wide_b - half_b))

    def mine(yo, zo, start, size):
        row = pl.multiple_of(index(yo, zo) * rows, rows)
        return p_ref.at[pl.ds(row, rows), pl.ds(start, size)]

    def copy(src, dst, target, s_sem, r_sem):
        return pltpu.make_async_remote_copy(
            src_ref=src, dst_ref=dst, send_sem=s_sem, recv_sem=r_sem,
            device_id={"dp": index(*target)}, device_id_type=MESH,
        )

    side = ((1, 0), (-1, 0))
    onward = ((0, 1), (0, -1))

    def toward(way, m):
        return m if way == 0 else -m

    def cell(way, m):
        return 2 * m - 1 + way

    def far_copy(zo, c, part):
        start, size = halves_a[part]
        return copy(mine(2, zo, start, size), far.at[c, :, pl.ds(start, size)], side[part],
                    far_s.at[c, part], far_r.at[c, part])

    def near_copy(c, part):
        return copy(near_out.at[c, part], near.at[c, part], side[part],
                    near_s.at[c, part], near_r.at[c, part])

    def stage_1(zo, c):
        for part in (0, 1):
            far_copy(zo, c, part).start()

    def stage_2(zo, c):
        for part in (0, 1):
            start, size = halves_a[part]
            rest, rest_size = halves_a[1 - part]
            yo = 1 if part == 0 else -1
            near_out[c, part, :, pl.ds(rest, rest_size)] = mine(yo, zo, rest, rest_size)[...]
            far_copy(zo, c, part).wait_recv()
            total = mine(yo, zo, start, size)[...].astype(f32) + far[c, :, pl.ds(start, size)].astype(f32)
            near_out[c, part, :, pl.ds(start, size)] = total.astype(bf16)
            near_copy(c, part).start()

    def stage_3(zo, c):
        for part in (0, 1):
            near_copy(c, part).wait_recv()
        return (mine(0, zo, 0, cut)[...].astype(f32) + near[c, 0].astype(f32)) + near[c, 1].astype(f32)

    def za_copy(way, m):
        return copy(za_out.at[way, m], za_in.at[way, m], onward[way], za_s.at[way, m], za_r.at[way, m])

    def zb_copy(way, m, stream, src=None):
        return copy(zb_out.at[way, m, stream] if src is None else src, zb_in.at[way, m, stream],
                    onward[way], zb_s.at[way, m, stream], zb_r.at[way, m, stream])

    def cells(m, known):
        if known and m == 0:
            return ((0, 0),)
        return tuple((toward(way, m), cell(way, m)) for way in (0, 1)
                     if not known or m <= reach(nz, "a", way))

    def ahead(m, known, stage):
        for zo, c in cells(m, known):
            stage(zo, c)

    def z_step(m, known):
        for stream in (0, 1, 2, 3):
            for way in (0, 1):
                limit = reach(nz, stream, way)
                if known and m > limit:
                    continue
                block = mine(stream, toward(way, m), cut, wide_b)
                if known and m == limit:
                    zb_copy(way, m - 1, stream, block).start()
                else:
                    zb_copy(way, m, stream).wait_recv()
                    total = block[...].astype(f32) + zb_in[way, m, stream].astype(f32)
                    zb_out[way, m - 1, stream] = total.astype(bf16)
                    zb_copy(way, m - 1, stream).start()
        for way in (0, 1):
            limit = reach(nz, "a", way)
            if known and m > limit:
                continue
            total = stage_3(toward(way, m), cell(way, m))
            if not (known and m == limit):
                za_copy(way, m).wait_recv()
                total = total + za_in[way, m].astype(f32)
            za_out[way, m - 1] = total.astype(bf16)
            za_copy(way, m - 1).start()

    greet(index)
    ahead(top, True, stage_1)
    ahead(top - 1, True, stage_1)
    ahead(top - 2, True, stage_1)
    ahead(top, True, stage_2)
    ahead(top - 1, True, stage_2)

    def iterate(m, known):
        if not known or m >= 3:
            ahead(m - 3, known, stage_1)
        if not known or m >= 2:
            ahead(m - 2, known, stage_2)
        z_step(m, known)

    peeled = [m for m in range(top, 0, -1) if m >= top - 1 or m <= 3]
    for m in [m for m in peeled if m >= top - 1]:
        iterate(m, True)
    inner = (top - 2) - 4 + 1
    if inner > 0:
        def body(i, carry):
            iterate(top - 2 - i, False)
            return carry

        lax.fori_loop(0, inner, body, 0)
    for m in [m for m in peeled if m < top - 1]:
        iterate(m, True)

    def b_final(stream):
        total = mine(stream, 0, cut, wide_b)[...].astype(f32)
        for way in (0, 1):
            zb_copy(way, 0, stream).wait_recv()
            total = total + zb_in[way, 0, stream].astype(f32)
        return total

    def bf_copy(part):
        start, size = halves_b[part]
        return copy(b_sum.at[:, pl.ds(start, size)], b_far.at[:, pl.ds(start, size)], side[part],
                    bf_s.at[part], bf_r.at[part])

    def bn_copy(part):
        return copy(b_near_out.at[part], b_near.at[part], side[part], bn_s.at[part], bn_r.at[part])

    b_sum[...] = b_final(2).astype(bf16)
    for part in (0, 1):
        bf_copy(part).start()
    next_to = (b_final(1), b_final(3))
    own_b = b_final(0)
    for part in (0, 1):
        start, size = halves_b[part]
        rest, rest_size = halves_b[1 - part]
        bf_copy(part).wait_recv()
        total = next_to[part]
        b_near_out[part, :, pl.ds(rest, rest_size)] = total[:, rest:rest + rest_size].astype(bf16)
        b_near_out[part, :, pl.ds(start, size)] = (
            total[:, start:start + size] + b_far[:, pl.ds(start, size)].astype(f32)).astype(bf16)
        bn_copy(part).start()
    total = stage_3(0, 0)
    for way in (0, 1):
        za_copy(way, 0).wait_recv()
        total = total + za_in[way, 0].astype(f32)
    out_ref[:, pl.ds(0, cut)] = total
    for part in (0, 1):
        bn_copy(part).wait_recv()
    out_ref[:, pl.ds(cut, wide_b)] = (own_b + b_near[0].astype(f32)) + b_near[1].astype(f32)

    def drain_y(zo, c):
        for part in (0, 1):
            far_copy(zo, c, part).wait_send()
            near_copy(c, part).wait_send()

    def drain(m, known):
        ahead(m, known, drain_y)
        for way in (0, 1):
            for stream in (0, 1, 2, 3):
                if not known or m <= reach(nz, stream, way):
                    zb_copy(way, m - 1, stream).wait_send()
            if not known or m <= reach(nz, "a", way):
                za_copy(way, m - 1).wait_send()

    drain_y(0, 0)

    def drain_body(m, carry):
        drain(m, False)
        return carry

    lax.fori_loop(1, top, drain_body, 0)
    drain(top, True)
    for part in (0, 1):
        bf_copy(part).wait_send()
        bn_copy(part).wait_send()


def scatter_sum(whole, ranks):
    rows, cols = whole.shape[0] // ranks, whole.shape[1]
    nz = ranks // RING_Y
    tiles = cols // 128
    cut = 128 * max(2, round(tiles * 0.633 + 0.2))
    half_a = 128 * ((cut // 128 + 1) // 2)
    wide_b = cols - cut
    half_b = 128 * ((wide_b // 128 + 1) // 2)
    k = nz // 2 + 1
    bf16 = jnp.bfloat16
    dma = pltpu.SemaphoreType.DMA
    return pl.pallas_call(
        functools.partial(scatter_kernel, nz, cut, half_a, half_b),
        out_shape=jax.ShapeDtypeStruct((rows, cols), jnp.float32),
        in_specs=[VMEM],
        out_specs=VMEM,
        scratch_shapes=[
            pltpu.VMEM((nz, rows, cut), bf16),
            pltpu.VMEM((nz, 2, rows, cut), bf16),
            pltpu.VMEM((nz, 2, rows, cut), bf16),
            pltpu.VMEM((2, k, rows, cut), bf16),
            pltpu.VMEM((2, k, rows, cut), bf16),
            pltpu.VMEM((2, k, 4, rows, wide_b), bf16),
            pltpu.VMEM((2, k, 4, rows, wide_b), bf16),
            pltpu.VMEM((rows, wide_b), bf16),
            pltpu.VMEM((rows, wide_b), bf16),
            pltpu.VMEM((2, rows, wide_b), bf16),
            pltpu.VMEM((2, rows, wide_b), bf16),
            dma((nz, 2)), dma((nz, 2)), dma((nz, 2)), dma((nz, 2)),
            dma((2, k)), dma((2, k)), dma((2, k, 4)), dma((2, k, 4)),
            dma((2,)), dma((2,)), dma((2,)), dma((2,)),
        ],
        compiler_params=pltpu.CompilerParams(
            collective_id=1, has_side_effects=True, vmem_limit_bytes=48 * 1024 * 1024),
        name="scatter_sum",
    )(whole)


def on_device(x_in, cotangent, w_gate, w_up, send_counts, recv_counts):
    ranks = lax.axis_size("dp")
    hidden = w_gate.shape[1]
    weights = gather_rows(jnp.concatenate([w_gate, w_up], axis=1), ranks)
    live_rows = BAL + jnp.sum(send_counts[0]) - jnp.sum(recv_counts[0])
    live = (jnp.arange(x_in.shape[0]) < live_rows)[:, None]
    both = jnp.dot(x_in, weights, preferred_element_type=jnp.float32)
    gate_val, up_val = both[:, :hidden], both[:, hidden:]
    sig = jax.nn.sigmoid(gate_val)
    cot_val = cotangent.astype(jnp.float32)
    d_gate = jnp.where(
        live, cot_val * up_val * sig * (1.0 + gate_val * (1.0 - sig)), 0.0
    ).astype(jnp.bfloat16)
    d_up = jnp.where(live, cot_val * gate_val * sig, 0.0).astype(jnp.bfloat16)
    whole = lax.dot_general(
        x_in, d_gate, (((0,), (0,)), ((), ())), preferred_element_type=jnp.float32
    ).astype(jnp.bfloat16)
    partial_value = lax.dot_general(
        jnp.concatenate([d_gate, d_up], axis=1), weights, (((1,), (1,)), ((), ())),
        preferred_element_type=jnp.float32,
    ).astype(jnp.bfloat16)
    partial_value, whole = lax.optimization_barrier((partial_value, whole))
    grad_x = lax.psum_scatter(partial_value, "mp", scatter_dimension=1, tiled=True)
    grad_gate = scatter_sum(whole, ranks)
    return (grad_x, grad_gate)


def solution(mesh):
    return jax.shard_map(
        on_device,
        mesh=mesh,
        in_specs=(
            P("dp", None),
            P("dp", "mp"),
            P("dp", "mp"),
            P("dp", "mp"),
            P("dp", None),
            P("dp", None),
        ),
        out_specs=(P("dp", "mp"), P("dp", "mp")),
        check_vma=False,
    )
```

time: 1060 us -> 147 us (0.14)
  the two profiles are of different devices: /device:TPU:1 before, /device:TPU:2 now
where the time goes in v2:
time: 147 us
  Pallas kernels  109 us (74%)
  between operations  15.4 us (10%)
  matrix products  14.5 us (10%)
  other arithmetic  5.1 us (3%)
  local copies, waits for them, and re-layouts  2.71 us (2%)
    pallas_call x1, Pallas kernels, gather_rows(): pl.pallas_call(functools.partial(gather_kernel, nz, cut, half_a, half_b),...  64.3 us
    pallas_call x1, Pallas kernels, scatter_sum(): pl.pallas_call(functools.partial(scatter_kernel, nz, cut, half_a, half_b)...  44.6 us
    dot_general x1, matrix products, on_device(): both = jnp.dot(x_in, weights, preferred_element_type=jnp.float32)  5.85 us
    dot_general x1, matrix products, on_device(): lax.dot_general(jnp.concatenate([d_gate, d_up], axis=1), weights, (((1,),...  4.35 us
    dot_general x1, matrix products, on_device(): lax.dot_general(x_in, d_gate, (((0,), (0,)), ((), ())), preferred_element...  4.3 us
  transfers between devices with their start and end apart: 1, of which 0 were waited for; matrix products, arithmetic and copies ran while one was open for 0% of the time, Pallas kernels for 30%

profile of v2, /device:TPU:2, one launch (start us, length us, event | category | flops | bytes accessed | tf_op | source)
XLA Modules:
  0.0 146.7 jit_solution(3855793148178751595)
XLA Ops:
  7.2 0.0 copy-start
  7.2 0.0 reduce-scatter.2.cloned.1.call-start
  7.2 1.4 reduce_sum.19
  8.6 1.3 reduce_sum.18
  11.2 1.5 %pad_maximum_fusion.w_ref = bf16[32,1792]{1,0:T(8,128)(2,1)} fusion(bf16[32,896]{1,0:T(8,128)(2,1)} %param.9, bf16[32,896]{1,0:T(8,128)(2,1)} %param.8), kind=kLoop, calls=%fused_computation.16 | loop fusion | flops 229376 | bytes 229376 | tf_op jit(solution)/shard_map/concatenate | solution.py:458
  12.7 64.3 %gather_rows.1 = bf16[2048,1792]{1,0:T(8,128)(2,1)} custom-call(bf16[32,1792]{1,0:T(8,128)(2,1)} %pad_maximum_fusion.w_ref), custom_call_target="tpu_custom_call" | custom-call | tf_op jit(solution)/shard_map/gather_rows/pallas_call | solution.py:208
  77.0 0.0 copy-done
  77.0 0.0 copy-start.2
  77.0 5.8 %convolution_bitcast_fusion = f32[400,1792]{1,0:T(8,128)S(1)} fusion(bf16[400,2048]{1,0:T(8,128)(2,1)S(1)} %copy-done, bf16[2048,1792]{1,0:T(8,128)(2,1)} %gather_rows.1), kind=kOutput, calls=%fused_computation.1 | convolution fusion | flops 2936012800 | bytes 11845632 | tf_op jit(solution)/shard_map/dot_general | solution.py:461
  82.9 0.0 copy-done.2
  82.9 0.0 slice-start
  82.9 0.9 fusion.3
  83.8 0.0 slice-start.1
  83.8 4.3 %convert_bitcast_fusion.p_ref = bf16[2048,896]{1,0:T(8,128)(2,1)} fusion(bf16[400,896]{1,0:T(8,128)(2,1)S(1)} %get-tuple-element.6, bf16[400,2048]{1,0:T(8,128)(2,1)S(1)} %copy-done), kind=kOutput, calls=%fused_computation | convolution fusion | flops 1469841408 | bytes 6025216 | tf_op jit(solution)/shard_map/dot_general | solution.py:469
  88.1 0.0 slice-done
  88.1 0.0 slice-done.1
  88.1 4.3 %convolution_convert_fusion = bf16[400,2048]{1,0:T(8,128)(2,1)} fusion(bf16[2048,1792]{1,0:T(8,128)(2,1)S(1)} %bitcast.10, bf16[400,896]{1,0:T(8,128)(2,1)S(1)} %get-tuple-element.7, bf16[400,896]{1,0:T(8,128)(2,1)S(1)} %get-tuple-element.6), kind=kOutput, calls=%fused_computation.2 | convolution fusion | flops 2939699200 | bytes 10412032 | tf_op jit(solution)/shard_map/dot_general | solution.py:472
  92.5 0.0 reduce-scatter.2.cloned.1.call-update
  92.5 0.0 copy-start.1
  92.5 2.0 %copy-done.1 = bf16[2048,896]{1,0:T(8,128)(2,1)S(1)} copy-done((bf16[2048,896]{1,0:T(8,128)(2,1)S(1)}, bf16[2048,896]{1,0:T(8,128)(2,1)}, u32[]{:S(2)}) %copy-start.1) | copy-done | bytes 3670040
  94.5 44.6 %scatter_sum.1 = f32[32,896]{1,0:T(8,128)S(1)} custom-call(bf16[2048,896]{1,0:T(8,128)(2,1)S(1)} %copy-done.1), custom_call_target="tpu_custom_call" | custom-call | tf_op jit(solution)/shard_map/scatter_sum/pallas_call | solution.py:428
  139.2 0.0 reduce-scatter.2.cloned.1.call-done
  139.2 0.6 copy.11
  (2 shorter events, 0.0 us)
Async XLA Ops:
  7.2 69.9 %copy-start = (bf16[400,2048]{1,0:T(8,128)(2,1)S(1)}, bf16[400,2048]{1,0:T(8,128)(2,1)}, u32[]{:S(2)}) copy-start(bf16[400,2048]{1,0:T(8,128)(2,1)} %param.6) | copy-start | bytes 4915204
  7.2 132.0 %reduce-scatter.2.cloned.1.call-start = ((), (), s32[]{:S(2)}) async-start(), calls=%async_computation.1 | async-start | bytes 1843200 | tf_op jit(solution)/shard_map/reduce_scatter | solution.py:477
  77.0 5.9 %copy-start.2 = (bf16[400,896]{1,0:T(8,128)(2,1)S(1)}, bf16[400,896]{1,0:T(8,128)(2,1)}, u32[]{:S(2)}) copy-start(bf16[400,896]{1,0:T(8,128)(2,1)} %param.7) | copy-start | bytes 2150404
  82.9 5.2 %slice-start = ((s8[7340032]{0:T(1024)(128)(4,1)}), s8[4194304]{0:T(1024)(128)(4,1)S(1)}, s32[]{:S(2)}) async-start(s8[7340032]{0:T(1024)(128)(4,1)} %bitcast.9), calls=%async_computation.2 | async-start | bytes 8388608
  83.8 4.3 %slice-start.1 = ((s8[7340032]{0:T(1024)(128)(4,1)}), s8[3145728]{0:T(1024)(128)(4,1)S(1)}, s32[]{:S(2)}) async-start(s8[7340032]{0:T(1024)(128)(4,1)} %bitcast.9), calls=%async_computation.3 | async-start | bytes 6291456
  92.5 2.0 %copy-start.1 = (bf16[2048,896]{1,0:T(8,128)(2,1)S(1)}, bf16[2048,896]{1,0:T(8,128)(2,1)}, u32[]{:S(2)}) copy-start(bf16[2048,896]{1,0:T(8,128)(2,1)} %convert_bitcast_fusion.p_ref) | copy-start | bytes 11010052
Sparse Core Ops, SparseCore 0:
  92.6 33.5 reduce-scatter.1

commit v3 on v2

--- a/solution.py
+++ b/solution.py
@@ -23,13 +23,15 @@
     return index
 
 
-def greet(index):
+def greet(index, peers=()):
     barrier = pltpu.get_barrier_semaphore()
+    for peer in peers:
+        pl.semaphore_signal(barrier, inc=1, device_id={"mp": peer}, device_id_type=MESH)
     for yo, zo in ((0, 1), (0, -1), (1, 0), (-1, 0)):
         pl.semaphore_signal(
             barrier, inc=1, device_id={"dp": index(yo, zo)}, device_id_type=MESH
         )
-    pl.semaphore_wait(barrier, 4)
+    pl.semaphore_wait(barrier, 4 + len(peers))
 
 
 def reach(nz, stream, way):
@@ -38,7 +40,8 @@
 
 
 def gather_kernel(
-    nz, cut, half_a, half_b, w_ref, out_ref, za_s, za_r, zb_s, zb_r, ya_s, ya_r, yb_s, yb_r, own
+    nz, cut, half_a, half_b, gate_ref, up_ref, sent_ref, got_ref, out_ref, live_ref,
+    w_ref, za_s, za_r, zb_s, zb_r, ya_s, ya_r, yb_s, yb_r, own
 ):
     index = place(nz)
     rows, cols = w_ref.shape
@@ -110,6 +113,11 @@
             y_wait(kind, zo, c, part)
             y_copy(kind, zo, c, part + 2).start()
 
+    hidden = gate_ref.shape[1]
+    w_ref[:, pl.ds(0, hidden)] = gate_ref[...]
+    w_ref[:, pl.ds(hidden, hidden)] = up_ref[...]
+    change = jnp.sum((sent_ref[...] - got_ref[...]).astype(jnp.float32), axis=1, keepdims=True)
+    live_ref[...] = jnp.broadcast_to(change + BAL, live_ref.shape)
     greet(index)
     keep = pltpu.make_async_copy(w_ref, out_ref.at[pl.ds(pl.multiple_of(index(0, 0) * rows, rows), rows), :], own)
     keep.start()
@@ -117,57 +125,64 @@
         y_copy("b", 0, 0, part, True).start()
     for way in (0, 1):
         z_copy("a", way, 1, True).start()
+    for part in (0, 1):
+        y_copy("a", 0, 0, part, True).start()
+    for way in (0, 1):
         z_copy(0, way, 1, True).start()
-    for part in (0, 1):
-        y_copy("a", 0, 0, part, True).start()
+
+    def move(stream, way, k, known):
+        if known and k > reach(nz, stream, way):
+            return False
+        z_wait(stream, way, k)
+        if not known or k + 1 <= reach(nz, stream, way):
+            z_copy(stream, way, k + 1).start()
+        return True
+
+    def a_step(k, known):
+        for way in (0, 1):
+            if move("a", way, k, known):
+                for part in (0, 1):
+                    y_copy("a", origin(way, k), cell(way, k), part).start()
+
+    def a_pass(k, known):
+        for way in (0, 1):
+            if not known or k <= reach(nz, "a", way):
+                y_pass("a", origin(way, k), cell(way, k))
+
+    def b_step(k, known):
+        for stream in (0, 3, 1, 2):
+            for way in (0, 1):
+                move(stream, way, k, known)
+
+    a_step(1, True)
     for part in (0, 1):
         y_wait("b", 0, 0, part)
         y_copy("b", 0, 0, part + 2).start()
         for way in (0, 1):
             z_copy(3 if part == 0 else 1, way, 1).start()
-
-    def step(k, known, first=False):
-        def arrives(stream, way):
-            return not known or k <= reach(nz, stream, way)
-
-        def goes_on(stream, way):
-            return not known or k + 1 <= reach(nz, stream, way)
-
-        for way in (0, 1):
-            if arrives("a", way):
-                z_wait("a", way, k)
-                if goes_on("a", way):
-                    z_copy("a", way, k + 1).start()
-                for part in (0, 1):
-                    y_copy("a", origin(way, k), cell(way, k), part).start()
-        if first:
-            for part in (2, 3):
-                y_wait("b", 0, 0, part)
-            for way in (0, 1):
-                z_copy(2, way, 1).start()
-        for stream in (0, 3, 1, 2):
-            for way in (0, 1):
-                if arrives(stream, way):
-                    z_wait(stream, way, k)
-                    if goes_on(stream, way):
-                        z_copy(stream, way, k + 1).start()
-        if first:
-            y_pass("a", 0, 0)
-        else:
-            for way in (0, 1):
-                y_pass("a", origin(way, k - 1), cell(way, k - 1))
-
-    step(1, True, True)
-    if top > 3:
-        def body(k, carry):
-            step(k, False)
-            return carry
-
-        lax.fori_loop(2, top - 1, body, 0)
-    if top > 2:
-        step(top - 1, True)
-    step(top, True)
-    y_pass("a", -top, cell(0, top))
+    y_pass("a", 0, 0)
+    a_step(2, top > 2 and 2 >= top - 1 or top == 2)
+    for part in (2, 3):
+        y_wait("b", 0, 0, part)
+    for way in (0, 1):
+        z_copy(2, way, 1).start()
+    a_pass(1, True)
+
+    def body(k, carry):
+        a_step(k, False)
+        b_step(k - 2, False)
+        a_pass(k - 1, False)
+        return carry
+
+    if top > 4:
+        lax.fori_loop(3, top - 1, body, 0)
+    for k in range(max(3, top - 1), top + 1):
+        a_step(k, True)
+        b_step(k - 2, True)
+        a_pass(k - 1, True)
+    a_pass(top, True)
+    b_step(top - 1, True)
+    b_step(top, True)
 
     def drain_y(c, zo):
         for part in (2, 3):
@@ -196,8 +211,8 @@
     keep.wait()
 
 
-def gather_rows(shard, ranks):
-    rows, cols = shard.shape
+def gather_rows(w_gate, w_up, sent, got, ranks):
+    rows, cols = w_gate.shape[0], 2 * w_gate.shape[1]
     nz = ranks // RING_Y
     tiles = cols // 128
     cut = 128 * max(2, round(tiles * 0.633))
@@ -207,22 +222,26 @@
     k = nz // 2 + 1
     return pl.pallas_call(
         functools.partial(gather_kernel, nz, cut, half_a, half_b),
-        out_shape=jax.ShapeDtypeStruct((ranks * rows, cols), shard.dtype),
-        in_specs=[VMEM],
-        out_specs=pl.BlockSpec(memory_space=pl.ANY),
+        out_shape=(
+            jax.ShapeDtypeStruct((ranks * rows, cols), w_gate.dtype),
+            jax.ShapeDtypeStruct((8, 128), jnp.float32),
+        ),
+        in_specs=[VMEM] * 4,
+        out_specs=(pl.BlockSpec(memory_space=pl.ANY), VMEM),
         scratch_shapes=[
+            pltpu.VMEM((rows, cols), w_gate.dtype),
             dma((2, k)), dma((2, k)), dma((2, k, 4)), dma((2, k, 4)),
             dma((nz, 4)), dma((nz, 4)), dma((4,)), dma((4,)), dma,
         ],
         compiler_params=pltpu.CompilerParams(collective_id=0, has_side_effects=True),
         name="gather_rows",
-    )(shard)
+    )(w_gate, w_up, sent, got)
 
 
 def scatter_kernel(
-    nz, cut, half_a, half_b, p_ref, out_ref,
+    nz, peers, cut, half_a, half_b, p_ref, d_ref, weights_ref, out_ref, grad_x_ref, part_out, part_in,
     far, near, near_out, za_in, za_out, zb_in, zb_out, b_sum, b_far, b_near, b_near_out,
-    far_s, far_r, near_s, near_r, za_s, za_r, zb_s, zb_r, bf_s, bf_r, bn_s, bn_r,
+    part_s, part_r, far_s, far_r, near_s, near_r, za_s, za_r, zb_s, zb_r, bf_s, bf_r, bn_s, bn_r,
 ):
     index = place(nz)
     rows, cols = out_ref.shape
@@ -297,7 +316,7 @@
         for zo, c in cells(m, known):
             stage(zo, c)
 
-    def z_step(m, known):
+    def b_step(m, known):
         for stream in (0, 1, 2, 3):
             for way in (0, 1):
                 limit = reach(nz, stream, way)
@@ -311,6 +330,8 @@
                     total = block[...].astype(f32) + zb_in[way, m, stream].astype(f32)
                     zb_out[way, m - 1, stream] = total.astype(bf16)
                     zb_copy(way, m - 1, stream).start()
+
+    def a_step(m, known):
         for way in (0, 1):
             limit = reach(nz, "a", way)
             if known and m > limit:
@@ -322,22 +343,47 @@
             za_out[way, m - 1] = total.astype(bf16)
             za_copy(way, m - 1).start()
 
-    greet(index)
+    group = lax.axis_index("mp")
+    width = grad_x_ref.shape[1]
+
+    def part_copy(i):
+        return pltpu.make_async_remote_copy(
+            src_ref=part_out.at[i], dst_ref=part_in.at[i], send_sem=part_s.at[i], recv_sem=part_r.at[i],
+            device_id={"mp": lax.rem(group + i, peers)}, device_id_type=MESH,
+        )
+
+    def share(i):
+        row = pl.multiple_of(lax.rem(group + i, peers) * width, width)
+        part_out[i] = lax.dot_general(
+            d_ref[...], weights_ref[pl.ds(row, width), :], (((1,), (1,)), ((), ())),
+            preferred_element_type=f32,
+        ).astype(bf16)
+
+    def share_out(i):
+        share(i)
+        part_copy(i).start()
+
+    greet(index, [lax.rem(group + i, peers) for i in range(1, peers)])
+    b_step(top, True)
     ahead(top, True, stage_1)
     ahead(top - 1, True, stage_1)
     ahead(top - 2, True, stage_1)
     ahead(top, True, stage_2)
+    b_step(top - 1, True)
     ahead(top - 1, True, stage_2)
 
     def iterate(m, known):
         if not known or m >= 3:
+            b_step(m - 2, known)
             ahead(m - 3, known, stage_1)
         if not known or m >= 2:
             ahead(m - 2, known, stage_2)
-        z_step(m, known)
-
-    peeled = [m for m in range(top, 0, -1) if m >= top - 1 or m <= 3]
-    for m in [m for m in peeled if m >= top - 1]:
+        a_step(m, known)
+        i = top + 1 - m
+        if not known or i < peers:
+            share_out(i)
+
+    for m in (top, top - 1):
         iterate(m, True)
     inner = (top - 2) - 4 + 1
     if inner > 0:
@@ -346,7 +392,7 @@
             return carry
 
         lax.fori_loop(0, inner, body, 0)
-    for m in [m for m in peeled if m < top - 1]:
+    for m in range(min(top - 2, 3), 2, -1):
         iterate(m, True)
 
     def b_final(stream):
@@ -367,6 +413,7 @@
     b_sum[...] = b_final(2).astype(bf16)
     for part in (0, 1):
         bf_copy(part).start()
+    iterate(2, True)
     next_to = (b_final(1), b_final(3))
     own_b = b_final(0)
     for part in (0, 1):
@@ -378,6 +425,15 @@
         b_near_out[part, :, pl.ds(start, size)] = (
             total[:, start:start + size] + b_far[:, pl.ds(start, size)].astype(f32)).astype(bf16)
         bn_copy(part).start()
+    iterate(1, True)
+    for i in range(top + 1, peers):
+        share_out(i)
+    share(0)
+    grad_x = part_out[0].astype(f32)
+    for i in range(1, peers):
+        part_copy(i).wait_recv()
+        grad_x = grad_x + part_in[i].astype(f32)
+    grad_x_ref[...] = grad_x.astype(bf16)
     total = stage_3(0, 0)
     for way in (0, 1):
         za_copy(way, 0).wait_recv()
@@ -412,9 +468,11 @@
     for part in (0, 1):
         bf_copy(part).wait_send()
         bn_copy(part).wait_send()
-
-
-def scatter_sum(whole, ranks):
+    for i in range(1, peers):
+        part_copy(i).wait_send()
+
+
+def scatter_sum(whole, d_both, weights, ranks, peers):
     rows, cols = whole.shape[0] // ranks, whole.shape[1]
     nz = ranks // RING_Y
     tiles = cols // 128
@@ -423,14 +481,20 @@
     wide_b = cols - cut
     half_b = 128 * ((wide_b // 128 + 1) // 2)
     k = nz // 2 + 1
+    tokens, width = d_both.shape[0], weights.shape[0] // peers
     bf16 = jnp.bfloat16
     dma = pltpu.SemaphoreType.DMA
     return pl.pallas_call(
-        functools.partial(scatter_kernel, nz, cut, half_a, half_b),
-        out_shape=jax.ShapeDtypeStruct((rows, cols), jnp.float32),
-        in_specs=[VMEM],
-        out_specs=VMEM,
+        functools.partial(scatter_kernel, nz, peers, cut, half_a, half_b),
+        out_shape=(
+            jax.ShapeDtypeStruct((rows, cols), jnp.float32),
+            jax.ShapeDtypeStruct((tokens, width), bf16),
+        ),
+        in_specs=[VMEM] * 3,
+        out_specs=(VMEM, VMEM),
         scratch_shapes=[
+            pltpu.VMEM((peers, tokens, width), bf16),
+            pltpu.VMEM((peers, tokens, width), bf16),
             pltpu.VMEM((nz, rows, cut), bf16),
             pltpu.VMEM((nz, 2, rows, cut), bf16),
             pltpu.VMEM((nz, 2, rows, cut), bf16),
@@ -442,6 +506,7 @@
             pltpu.VMEM((rows, wide_b), bf16),
             pltpu.VMEM((2, rows, wide_b), bf16),
             pltpu.VMEM((2, rows, wide_b), bf16),
+            dma((peers,)), dma((peers,)),
             dma((nz, 2)), dma((nz, 2)), dma((nz, 2)), dma((nz, 2)),
             dma((2, k)), dma((2, k)), dma((2, k, 4)), dma((2, k, 4)),
             dma((2,)), dma((2,)), dma((2,)), dma((2,)),
@@ -449,15 +514,14 @@
         compiler_params=pltpu.CompilerParams(
             collective_id=1, has_side_effects=True, vmem_limit_bytes=48 * 1024 * 1024),
         name="scatter_sum",
-    )(whole)
+    )(whole, d_both, weights)
 
 
 def on_device(x_in, cotangent, w_gate, w_up, send_counts, recv_counts):
     ranks = lax.axis_size("dp")
     hidden = w_gate.shape[1]
-    weights = gather_rows(jnp.concatenate([w_gate, w_up], axis=1), ranks)
-    live_rows = BAL + jnp.sum(send_counts[0]) - jnp.sum(recv_counts[0])
-    live = (jnp.arange(x_in.shape[0]) < live_rows)[:, None]
+    weights, live_rows = gather_rows(w_gate, w_up, send_counts, recv_counts, ranks)
+    live = (lax.broadcasted_iota(jnp.float32, (x_in.shape[0], 1), 0) < live_rows[0, 0])
     both = jnp.dot(x_in, weights, preferred_element_type=jnp.float32)
     gate_val, up_val = both[:, :hidden], both[:, hidden:]
     sig = jax.nn.sigmoid(gate_val)
@@ -469,13 +533,8 @@
     whole = lax.dot_general(
         x_in, d_gate, (((0,), (0,)), ((), ())), preferred_element_type=jnp.float32
     ).astype(jnp.bfloat16)
-    partial_value = lax.dot_general(
-        jnp.concatenate([d_gate, d_up], axis=1), weights, (((1,), (1,)), ((), ())),
-        preferred_element_type=jnp.float32,
-    ).astype(jnp.bfloat16)
-    partial_value, whole = lax.optimization_barrier((partial_value, whole))
-    grad_x = lax.psum_scatter(partial_value, "mp", scatter_dimension=1, tiled=True)
-    grad_gate = scatter_sum(whole, ranks)
+    grad_gate, grad_x = scatter_sum(
+        whole, jnp.concatenate([d_gate, d_up], axis=1), weights, ranks, lax.axis_size("mp"))
     return (grad_x, grad_gate)
 
 

time: 147 us -> 123 us (0.84)
  the two profiles are of different devices: /device:TPU:2 before, /device:TPU:1 now
where the time goes in v3:
time: 123 us
  Pallas kernels  110 us (89%)
  matrix products  8.24 us (7%)
  local copies, waits for them, and re-layouts  2.52 us (2%)
  other arithmetic  1.66 us (1%)
    pallas_call x1, Pallas kernels, gather_rows(): pl.pallas_call(functools.partial(gather_kernel, nz, cut, half_a, half_b),...  61 us
    pallas_call x1, Pallas kernels, scatter_sum(): pl.pallas_call(functools.partial(scatter_kernel, nz, peers, cut, half_a,...  48.8 us
    dot_general x1, matrix products, on_device(): both = jnp.dot(x_in, weights, preferred_element_type=jnp.float32)  5.85 us

profile of v3, /device:TPU:1, one launch (start us, length us, event | category | flops | bytes accessed | tf_op | source)
XLA Modules:
  0.0 123.0 jit_solution(12480759119501378780)
XLA Ops:
  0.6 0.0 copy-start
  0.6 61.0 %gather_rows.1 = (bf16[2048,1792]{1,0:T(8,128)(2,1)}, f32[8,128]{1,0:T(8,128)}) custom-call(bf16[32,896]{1,0:T(8,128)(2,1)} %gate_ref.1, bf16[32,896]{1,0:T(8,128)(2,1)} %up_ref.1, s32[1,64]{1,0:T(1,128)} %sent_ref.1, s32[1,64]{1,0:T(1,128)} %got_ref.1), custom_call_target="tpu_custom_call" | custom-call | tf_op jit(solution)/shard_map/gather_rows/pallas_call | solution.py:223
  61.7 1.2 slice.9
  62.9 0.7 iota_compare_fusion
  63.5 0.0 copy-done
  63.5 0.0 copy-start.1
  63.5 5.8 %convolution_bitcast_fusion = f32[400,1792]{1,0:T(8,128)S(1)} fusion(bf16[400,2048]{1,0:T(8,128)(2,1)S(1)} %copy-done, bf16[2048,1792]{1,0:T(8,128)(2,1)} %get-tuple-element.7.weights_ref), kind=kOutput, calls=%fused_computation.1 | convolution fusion | flops 2936012800 | bytes 11845632 | tf_op jit(solution)/shard_map/dot_general | solution.py:525
  69.4 0.0 copy-done.1
  69.4 0.9 fusion.6
  70.3 0.1 pad_maximum_fusion.d_ref
  70.4 2.4 %convert_bitcast_fusion.p_ref = bf16[2048,896]{1,0:T(8,128)(2,1)S(1)} fusion(bf16[400,896]{1,0:T(8,128)(2,1)S(1)} %get-tuple-element.11, bf16[400,2048]{1,0:T(8,128)(2,1)S(1)} %copy-done), kind=kOutput, calls=%fused_computation | convolution fusion | flops 1469841408 | bytes 6025216 | tf_op jit(solution)/shard_map/dot_general | solution.py:533
  72.8 48.8 %scatter_sum.1 = (f32[32,896]{1,0:T(8,128)S(1)}, bf16[400,256]{1,0:T(8,128)(2,1)S(1)}) custom-call(bf16[2048,896]{1,0:T(8,128)(2,1)S(1)} %convert_bitcast_fusion.p_ref, bf16[400,1792]{1,0:T(8,128)(2,1)S(1)} %pad_maximum_fusion.d_ref, bf16[2048,1792]{1,0:T(8,128)(2,1)} %get-tuple-element.7.weights_ref), custom_call_target="tpu_custom_call" | custom-call | tf_op jit(solution)/shard_map/scatter_sum/pallas_call | solution.py:487
  121.6 0.7 copy.12
  122.3 0.6 copy.13
Async XLA Ops:
  0.6 62.9 %copy-start = (bf16[400,2048]{1,0:T(8,128)(2,1)S(1)}, bf16[400,2048]{1,0:T(8,128)(2,1)}, u32[]{:S(2)}) copy-start(bf16[400,2048]{1,0:T(8,128)(2,1)} %param.6) | copy-start | bytes 4915204
  63.5 5.9 %copy-start.1 = (bf16[400,896]{1,0:T(8,128)(2,1)S(1)}, bf16[400,896]{1,0:T(8,128)(2,1)}, u32[]{:S(2)}) copy-start(bf16[400,896]{1,0:T(8,128)(2,1)} %param.7) | copy-start | bytes 2150404

commit v4 on v3

--- a/solution.py
+++ b/solution.py
@@ -40,7 +40,7 @@
 
 
 def gather_kernel(
-    nz, cut, half_a, half_b, gate_ref, up_ref, sent_ref, got_ref, out_ref, live_ref,
+    nz, cut, half_a, half_b, gate_ref, up_ref, sent_ref, got_ref, cot_ref, out_ref, cot_live_ref,
     w_ref, za_s, za_r, zb_s, zb_r, ya_s, ya_r, yb_s, yb_r, own
 ):
     index = place(nz)
@@ -49,6 +49,7 @@
     spans = {"a": (0, cut), "b": (cut, cols - cut)}
     halves = {
         "a": ((0, half_a), (half_a, cut - half_a)),
+        "a_odd": ((half_a, cut - half_a), (0, half_a)),
         "b": ((cut, half_b), (cut + half_b, cols - cut - half_b)),
     }
 
@@ -86,12 +87,12 @@
         copy(dst, dst, onward(way), other, sem).wait_recv()
 
     def y_sems(kind, c, part):
-        if kind == "a":
+        if kind != "b":
             return ya_s.at[c, part], ya_r.at[c, part]
         return yb_s.at[part], yb_r.at[part]
 
     def y_part(kind, part):
-        return spans[kind] if part < 2 else halves[kind][part - 2]
+        return spans[kind[0]] if part < 2 else halves[kind][part - 2]
 
     def y_copy(kind, zo, c, part, mine=False):
         span = y_part(kind, part)
@@ -108,6 +109,9 @@
     def cell(way, k):
         return 2 * k - 1 + way
 
+    def sort(way):
+        return ("a_odd", "a")[way]
+
     def y_pass(kind, zo, c):
         for part in (0, 1):
             y_wait(kind, zo, c, part)
@@ -116,8 +120,6 @@
     hidden = gate_ref.shape[1]
     w_ref[:, pl.ds(0, hidden)] = gate_ref[...]
     w_ref[:, pl.ds(hidden, hidden)] = up_ref[...]
-    change = jnp.sum((sent_ref[...] - got_ref[...]).astype(jnp.float32), axis=1, keepdims=True)
-    live_ref[...] = jnp.broadcast_to(change + BAL, live_ref.shape)
     greet(index)
     keep = pltpu.make_async_copy(w_ref, out_ref.at[pl.ds(pl.multiple_of(index(0, 0) * rows, rows), rows), :], own)
     keep.start()
@@ -142,17 +144,24 @@
         for way in (0, 1):
             if move("a", way, k, known):
                 for part in (0, 1):
-                    y_copy("a", origin(way, k), cell(way, k), part).start()
+                    y_copy(sort(way), origin(way, k), cell(way, k), part).start()
 
     def a_pass(k, known):
         for way in (0, 1):
             if not known or k <= reach(nz, "a", way):
-                y_pass("a", origin(way, k), cell(way, k))
+                y_pass(sort(way), origin(way, k), cell(way, k))
 
     def b_step(k, known):
         for stream in (0, 3, 1, 2):
             for way in (0, 1):
                 move(stream, way, k, known)
+
+    change = jnp.sum((sent_ref[...] - got_ref[...]).astype(jnp.float32), axis=1, keepdims=True)
+    row = lax.broadcasted_iota(jnp.int32, (cot_ref.shape[0], 128), 0).astype(jnp.float32)
+    live = row < jnp.broadcast_to(change + BAL, row.shape)
+    for start in range(0, cot_ref.shape[1], 128):
+        value = cot_ref[:, pl.ds(start, 128)].astype(jnp.float32)
+        cot_live_ref[:, pl.ds(start, 128)] = jnp.where(live, value, 0.0).astype(cot_live_ref.dtype)
 
     a_step(1, True)
     for part in (0, 1):
@@ -184,13 +193,13 @@
     b_step(top - 1, True)
     b_step(top, True)
 
-    def drain_y(c, zo):
+    def drain_y(kind, c, zo):
         for part in (2, 3):
-            y_wait("a", zo, c, part)
+            y_wait(kind, zo, c, part)
         for part in range(4):
-            y_copy("a", zo, c, part).wait_send()
-
-    drain_y(0, 0)
+            y_copy(kind, zo, c, part).wait_send()
+
+    drain_y("a", 0, 0)
     for part in range(4):
         y_copy("b", 0, 0, part).wait_send()
 
@@ -200,7 +209,7 @@
                 if not known or k <= reach(nz, stream, way):
                     z_copy(stream, way, k).wait_send()
             if not known or k <= reach(nz, "a", way):
-                drain_y(cell(way, k), origin(way, k))
+                drain_y(sort(way), cell(way, k), origin(way, k))
 
     def drain_body(k, carry):
         drain(k, False)
@@ -211,7 +220,7 @@
     keep.wait()
 
 
-def gather_rows(w_gate, w_up, sent, got, ranks):
+def gather_rows(w_gate, w_up, sent, got, cotangent, ranks):
     rows, cols = w_gate.shape[0], 2 * w_gate.shape[1]
     nz = ranks // RING_Y
     tiles = cols // 128
@@ -224,18 +233,19 @@
         functools.partial(gather_kernel, nz, cut, half_a, half_b),
         out_shape=(
             jax.ShapeDtypeStruct((ranks * rows, cols), w_gate.dtype),
-            jax.ShapeDtypeStruct((8, 128), jnp.float32),
+            jax.ShapeDtypeStruct(cotangent.shape, cotangent.dtype),
         ),
-        in_specs=[VMEM] * 4,
-        out_specs=(pl.BlockSpec(memory_space=pl.ANY), VMEM),
+        in_specs=[VMEM] * 5,
+        out_specs=(VMEM, VMEM),
         scratch_shapes=[
             pltpu.VMEM((rows, cols), w_gate.dtype),
             dma((2, k)), dma((2, k)), dma((2, k, 4)), dma((2, k, 4)),
             dma((nz, 4)), dma((nz, 4)), dma((4,)), dma((4,)), dma,
         ],
-        compiler_params=pltpu.CompilerParams(collective_id=0, has_side_effects=True),
+        compiler_params=pltpu.CompilerParams(
+            collective_id=0, has_side_effects=True, vmem_limit_bytes=20 * 1024 * 1024),
         name="gather_rows",
-    )(w_gate, w_up, sent, got)
+    )(w_gate, w_up, sent, got, cotangent)
 
 
 def scatter_kernel(
@@ -476,7 +486,7 @@
     rows, cols = whole.shape[0] // ranks, whole.shape[1]
     nz = ranks // RING_Y
     tiles = cols // 128
-    cut = 128 * max(2, round(tiles * 0.633 + 0.2))
+    cut = 128 * max(2, round(tiles * 0.55))
     half_a = 128 * ((cut // 128 + 1) // 2)
     wide_b = cols - cut
     half_b = 128 * ((wide_b // 128 + 1) // 2)
@@ -512,7 +522,7 @@
             dma((2,)), dma((2,)), dma((2,)), dma((2,)),
         ],
         compiler_params=pltpu.CompilerParams(
-            collective_id=1, has_side_effects=True, vmem_limit_bytes=48 * 1024 * 1024),
+            collective_id=1, has_side_effects=True, vmem_limit_bytes=32 * 1024 * 1024),
         name="scatter_sum",
     )(whole, d_both, weights)
 
@@ -520,16 +530,13 @@
 def on_device(x_in, cotangent, w_gate, w_up, send_counts, recv_counts):
     ranks = lax.axis_size("dp")
     hidden = w_gate.shape[1]
-    weights, live_rows = gather_rows(w_gate, w_up, send_counts, recv_counts, ranks)
-    live = (lax.broadcasted_iota(jnp.float32, (x_in.shape[0], 1), 0) < live_rows[0, 0])
+    weights, cot_live = gather_rows(w_gate, w_up, send_counts, recv_counts, cotangent, ranks)
     both = jnp.dot(x_in, weights, preferred_element_type=jnp.float32)
     gate_val, up_val = both[:, :hidden], both[:, hidden:]
     sig = jax.nn.sigmoid(gate_val)
-    cot_val = cotangent.astype(jnp.float32)
-    d_gate = jnp.where(
-        live, cot_val * up_val * sig * (1.0 + gate_val * (1.0 - sig)), 0.0
-    ).astype(jnp.bfloat16)
-    d_up = jnp.where(live, cot_val * gate_val * sig, 0.0).astype(jnp.bfloat16)
+    cot_val = cot_live.astype(jnp.float32)
+    d_gate = (cot_val * up_val * sig * (1.0 + gate_val * (1.0 - sig))).astype(jnp.bfloat16)
+    d_up = (cot_val * gate_val * sig).astype(jnp.bfloat16)
     whole = lax.dot_general(
         x_in, d_gate, (((0,), (0,)), ((), ())), preferred_element_type=jnp.float32
     ).astype(jnp.bfloat16)

time: 123 us -> 117 us (0.951)
  Pallas kernels: 110 us -> 104 us
  local copies, waits for them, and re-layouts: 2.52 us -> 5.51 us
  matrix products: 8.24 us -> 5.51 us
    unnamed x6 -> x14, local copies, waits for them, and re-layouts: 1.34 us -> 5.51 us
    pallas_call x1, Pallas kernels: 61 us -> 57.8 us  [gather_rows(): pl.pallas_call(functools.partial(gather_kernel, nz, cut, half_a, half_b),...]
    dot_general x1, matrix products: 5.85 us -> 3.11 us  [on_device(): both = jnp.dot(x_in, weights, preferred_element_type=jnp.float32)]
    pallas_call x1, Pallas kernels: 48.8 us -> 46.4 us  [scatter_sum(): pl.pallas_call(functools.partial(scatter_kernel, nz, peers, cut, half_a,...]
where the time goes in v4:
time: 117 us
  Pallas kernels  104 us (89%)
  local copies, waits for them, and re-layouts  5.51 us (5%)
  matrix products  5.51 us (5%)
    pallas_call x1, Pallas kernels, gather_rows(): pl.pallas_call(functools.partial(gather_kernel, nz, cut, half_a, half_b),...  57.8 us
    pallas_call x1, Pallas kernels, scatter_sum(): pl.pallas_call(functools.partial(scatter_kernel, nz, peers, cut, half_a,...  46.4 us
    unnamed x14, local copies, waits for them, and re-layouts  5.51 us
    dot_general x1, matrix products, on_device(): both = jnp.dot(x_in, weights, preferred_element_type=jnp.float32)  3.11 us
    dot_general x1, matrix products, on_device(): lax.dot_general(x_in, d_gate, (((0,), (0,)), ((), ())), preferred_element...  2.39 us

profile of v4, /device:TPU:1, one launch (start us, length us, event | category | flops | bytes accessed | tf_op | source)
XLA Modules:
  0.0 116.8 jit_solution(12131873034238336365)
XLA Ops:
  0.6 0.0 copy-start
  0.6 0.0 copy-start.1
  0.7 1.2 %copy-done.1 = bf16[400,896]{1,0:T(8,128)(2,1)S(1)} copy-done((bf16[400,896]{1,0:T(8,128)(2,1)S(1)}, bf16[400,896]{1,0:T(8,128)(2,1)}, u32[]{:S(2)}) %copy-start.1) | copy-done | bytes 716824
  1.9 0.0 copy-start.2
  1.9 0.8 copy-done.2
  2.7 0.0 copy-start.3
  2.7 0.8 copy-done.3
  3.5 0.0 copy-start.4
  3.5 0.7 copy-done.4
  4.2 0.0 copy-start.5
  4.2 0.7 copy-done.5
  4.8 57.8 %gather_rows.1 = (bf16[2048,1792]{1,0:T(8,128)(2,1)S(1)}, bf16[400,896]{1,0:T(8,128)(2,1)S(1)}) custom-call(bf16[32,896]{1,0:T(8,128)(2,1)S(1)} %copy-done.2, bf16[32,896]{1,0:T(8,128)(2,1)S(1)} %copy-done.3, s32[1,64]{1,0:T(1,128)S(1)} %copy-done.4, s32[1,64]{1,0:T(1,128)S(1)} %copy-done.5, bf16[400,896]{1,0:T(8,128)(2,1)S(1)} %copy-done.1), custom_call_target="tpu_custom_call" | custom-call | tf_op jit(solution)/shard_map/gather_rows/pallas_call | solution.py:232
  62.6 0.0 copy-done
  62.6 3.1 %convolution_bitcast_fusion = f32[400,1792]{1,0:T(8,128)S(1)} fusion(bf16[400,2048]{1,0:T(8,128)(2,1)S(1)} %copy-done, bf16[2048,1792]{1,0:T(8,128)(2,1)S(1)} %get-tuple-element.7.weights_ref), kind=kOutput, calls=%fused_computation.1 | convolution fusion | flops 2936012800 | bytes 11845632 | tf_op jit(solution)/shard_map/dot_general | solution.py:534
  65.8 0.7 fusion.4
  66.5 0.1 pad_maximum_fusion.d_ref
  66.6 2.4 %convert_bitcast_fusion.p_ref = bf16[2048,896]{1,0:T(8,128)(2,1)S(1)} fusion(bf16[400,896]{1,0:T(8,128)(2,1)S(1)} %get-tuple-element.11, bf16[400,2048]{1,0:T(8,128)(2,1)S(1)} %copy-done), kind=kOutput, calls=%fused_computation | convolution fusion | flops 1469841408 | bytes 6025216 | tf_op jit(solution)/shard_map/dot_general | solution.py:540
  69.0 46.4 %scatter_sum.1 = (f32[32,896]{1,0:T(8,128)S(1)}, bf16[400,256]{1,0:T(8,128)(2,1)S(1)}) custom-call(bf16[2048,896]{1,0:T(8,128)(2,1)S(1)} %convert_bitcast_fusion.p_ref, bf16[400,1792]{1,0:T(8,128)(2,1)S(1)} %pad_maximum_fusion.d_ref, bf16[2048,1792]{1,0:T(8,128)(2,1)S(1)} %get-tuple-element.7.weights_ref), custom_call_target="tpu_custom_call" | custom-call | tf_op jit(solution)/shard_map/scatter_sum/pallas_call | solution.py:497
  115.4 0.7 copy.12
  116.1 0.6 copy.13
Async XLA Ops:
  0.6 62.0 %copy-start = (bf16[400,2048]{1,0:T(8,128)(2,1)S(1)}, bf16[400,2048]{1,0:T(8,128)(2,1)}, u32[]{:S(2)}) copy-start(bf16[400,2048]{1,0:T(8,128)(2,1)} %param.6) | copy-start | bytes 4915204
  0.6 1.2 %copy-start.1 = (bf16[400,896]{1,0:T(8,128)(2,1)S(1)}, bf16[400,896]{1,0:T(8,128)(2,1)}, u32[]{:S(2)}) copy-start(bf16[400,896]{1,0:T(8,128)(2,1)} %cot_ref.1) | copy-start | bytes 2150404
  1.9 0.8 copy-start.2
  2.7 0.8 copy-start.3
  3.5 0.7 copy-start.4
  4.2 0.7 copy-start.5

commit v5 on v4

--- a/solution.py
+++ b/solution.py
@@ -11,6 +11,7 @@
 RING_Y = 4
 MESH = pl.DeviceIdType.MESH
 VMEM = pl.BlockSpec(memory_space=pltpu.VMEM)
+HBM = pl.BlockSpec(memory_space=pltpu.HBM)
 
 
 def place(nz):
@@ -40,8 +41,9 @@
 
 
 def gather_kernel(
-    nz, cut, half_a, half_b, gate_ref, up_ref, sent_ref, got_ref, cot_ref, out_ref, cot_live_ref,
-    w_ref, za_s, za_r, zb_s, zb_r, ya_s, ya_r, yb_s, yb_r, own
+    nz, cut, half_a, half_b, gate_ref, up_ref, sent_hbm, got_hbm, cot_hbm, out_ref, cot_live_ref,
+    w_ref, sent_ref, got_ref, cot_ref, fetched,
+    za_s, za_r, zb_s, zb_r, ya_s, ya_r, yb_s, yb_r, own
 ):
     index = place(nz)
     rows, cols = w_ref.shape
@@ -118,9 +120,21 @@
             y_copy(kind, zo, c, part + 2).start()
 
     hidden = gate_ref.shape[1]
-    w_ref[:, pl.ds(0, hidden)] = gate_ref[...]
-    w_ref[:, pl.ds(hidden, hidden)] = up_ref[...]
+    fetches = [
+        pltpu.make_async_copy(src, dst, fetched.at[i])
+        for i, (src, dst) in enumerate((
+            (gate_ref, w_ref.at[:, pl.ds(0, hidden)]),
+            (up_ref, w_ref.at[:, pl.ds(hidden, hidden)]),
+            (sent_hbm, sent_ref),
+            (got_hbm, got_ref),
+            (cot_hbm, cot_ref),
+        ))
+    ]
+    for fetch in fetches:
+        fetch.start()
     greet(index)
+    for fetch in fetches[:2]:
+        fetch.wait()
     keep = pltpu.make_async_copy(w_ref, out_ref.at[pl.ds(pl.multiple_of(index(0, 0) * rows, rows), rows), :], own)
     keep.start()
     for part in (0, 1):
@@ -156,6 +170,8 @@
             for way in (0, 1):
                 move(stream, way, k, known)
 
+    for fetch in fetches[2:]:
+        fetch.wait()
     change = jnp.sum((sent_ref[...] - got_ref[...]).astype(jnp.float32), axis=1, keepdims=True)
     row = lax.broadcasted_iota(jnp.int32, (cot_ref.shape[0], 128), 0).astype(jnp.float32)
     live = row < jnp.broadcast_to(change + BAL, row.shape)
@@ -235,17 +251,21 @@
             jax.ShapeDtypeStruct((ranks * rows, cols), w_gate.dtype),
             jax.ShapeDtypeStruct(cotangent.shape, cotangent.dtype),
         ),
-        in_specs=[VMEM] * 5,
+        in_specs=[HBM] * 5,
         out_specs=(VMEM, VMEM),
         scratch_shapes=[
             pltpu.VMEM((rows, cols), w_gate.dtype),
+            pltpu.VMEM(sent.shape, sent.dtype),
+            pltpu.VMEM(got.shape, got.dtype),
+            pltpu.VMEM(cotangent.shape, cotangent.dtype),
+            dma((5,)),
             dma((2, k)), dma((2, k)), dma((2, k, 4)), dma((2, k, 4)),
             dma((nz, 4)), dma((nz, 4)), dma((4,)), dma((4,)), dma,
         ],
         compiler_params=pltpu.CompilerParams(
             collective_id=0, has_side_effects=True, vmem_limit_bytes=20 * 1024 * 1024),
         name="gather_rows",
-    )(w_gate, w_up, sent, got, cotangent)
+    )(*(pltpu.with_memory_space_constraint(a, pltpu.HBM) for a in (w_gate, w_up, sent, got, cotangent)))
 
 
 def scatter_kernel(
@@ -356,30 +376,61 @@
     group = lax.axis_index("mp")
     width = grad_x_ref.shape[1]
 
-    def part_copy(i):
+    chips = peers // 2
+    chip, core = lax.div(group, 2), lax.rem(group, 2)
+
+    def owner(j, same):
+        return lax.rem(chip + j, chips) * 2 + (core if same else 1 - core)
+
+    def part_copy(i, target):
         return pltpu.make_async_remote_copy(
             src_ref=part_out.at[i], dst_ref=part_in.at[i], send_sem=part_s.at[i], recv_sem=part_r.at[i],
-            device_id={"mp": lax.rem(group + i, peers)}, device_id_type=MESH,
+            device_id={"mp": target}, device_id_type=MESH,
         )
 
-    def share(i):
-        row = pl.multiple_of(lax.rem(group + i, peers) * width, width)
+    def chip_copy(j):
+        return part_copy(j, owner(j, True))
+
+    def pair_copy(j):
+        return part_copy(chips + j, owner(0, False))
+
+    def share(i, target):
+        row = pl.multiple_of(target * width, width)
         part_out[i] = lax.dot_general(
             d_ref[...], weights_ref[pl.ds(row, width), :], (((1,), (1,)), ((), ())),
             preferred_element_type=f32,
         ).astype(bf16)
 
-    def share_out(i):
-        share(i)
-        part_copy(i).start()
-
-    greet(index, [lax.rem(group + i, peers) for i in range(1, peers)])
+    def pair_sum(j):
+        pair_copy(j).wait_recv()
+        return part_out[j].astype(f32) + part_in[chips + j].astype(f32)
+
+    tour = sorted(range(chips), key=lambda j: -min(j, chips - j))
+    jobs = [(j, same) for j in tour for same in (False, True)]
+    ready = []
+
+    def advance():
+        if ready:
+            j = ready.pop(0)
+            part_out[j] = pair_sum(j).astype(bf16)
+            chip_copy(j).start()
+        if jobs:
+            j, same = jobs.pop(0)
+            share(j if same else chips + j, owner(j, same))
+            if not same:
+                pair_copy(j).start()
+            elif j:
+                ready.append(j)
+
+    greet(index, [owner(0, False)] + [owner(j, True) for j in range(1, chips)])
     b_step(top, True)
     ahead(top, True, stage_1)
     ahead(top - 1, True, stage_1)
     ahead(top - 2, True, stage_1)
+    advance()
     ahead(top, True, stage_2)
     b_step(top - 1, True)
+    advance()
     ahead(top - 1, True, stage_2)
 
     def iterate(m, known):
@@ -389,20 +440,9 @@
         if not known or m >= 2:
             ahead(m - 2, known, stage_2)
         a_step(m, known)
-        i = top + 1 - m
-        if not known or i < peers:
-            share_out(i)
-
-    for m in (top, top - 1):
-        iterate(m, True)
-    inner = (top - 2) - 4 + 1
-    if inner > 0:
-        def body(i, carry):
-            iterate(top - 2 - i, False)
-            return carry
-
-        lax.fori_loop(0, inner, body, 0)
-    for m in range(min(top - 2, 3), 2, -1):
+        advance()
+
+    for m in range(top, 2, -1):
         iterate(m, True)
 
     def b_final(stream):
@@ -436,13 +476,12 @@
             total[:, start:start + size] + b_far[:, pl.ds(start, size)].astype(f32)).astype(bf16)
         bn_copy(part).start()
     iterate(1, True)
-    for i in range(top + 1, peers):
-        share_out(i)
-    share(0)
-    grad_x = part_out[0].astype(f32)
-    for i in range(1, peers):
-        part_copy(i).wait_recv()
-        grad_x = grad_x + part_in[i].astype(f32)
+    while jobs or ready:
+        advance()
+    grad_x = pair_sum(0)
+    for j in range(1, chips):
+        chip_copy(j).wait_recv()
+        grad_x = grad_x + part_in[j].astype(f32)
     grad_x_ref[...] = grad_x.astype(bf16)
     total = stage_3(0, 0)
     for way in (0, 1):
@@ -478,8 +517,10 @@
     for part in (0, 1):
         bf_copy(part).wait_send()
         bn_copy(part).wait_send()
-    for i in range(1, peers):
-        part_copy(i).wait_send()
+    for j in range(chips):
+        pair_copy(j).wait_send()
+        if j:
+            chip_copy(j).wait_send()
 
 
 def scatter_sum(whole, d_both, weights, ranks, peers):

time: 117 us -> 111 us (0.949)
  the two profiles are of different devices: /device:TPU:1 before, /device:TPU:8 now
where the time goes in v5:
time: 111 us
  Pallas kernels  103 us (93%)
  matrix products  5.51 us (5%)
  local copies, waits for them, and re-layouts  1.34 us (1%)
    pallas_call x1, Pallas kernels, gather_rows(): pl.pallas_call(functools.partial(gather_kernel, nz, cut, half_a, half_b),...  58.8 us
    pallas_call x1, Pallas kernels, scatter_sum(): pl.pallas_call(functools.partial(scatter_kernel, nz, peers, cut, half_a,...  44.1 us
    dot_general x1, matrix products, on_device(): both = jnp.dot(x_in, weights, preferred_element_type=jnp.float32)  3.12 us
    dot_general x1, matrix products, on_device(): lax.dot_general(x_in, d_gate, (((0,), (0,)), ((), ())), preferred_element...  2.39 us

profile of v5, /device:TPU:8, one launch (start us, length us, event | category | flops | bytes accessed | tf_op | source)
XLA Modules:
  0.0 111.3 jit_solution(3531165002096949318)
XLA Ops:
  0.6 0.0 copy-start
  0.6 58.8 %gather_rows.1 = (bf16[2048,1792]{1,0:T(8,128)(2,1)S(1)}, bf16[400,896]{1,0:T(8,128)(2,1)S(1)}) custom-call(bf16[32,896]{1,0:T(8,128)(2,1)} %gate_ref.1, bf16[32,896]{1,0:T(8,128)(2,1)} %up_ref.1, s32[1,64]{1,0:T(1,128)} %sent_hbm.1, s32[1,64]{1,0:T(1,128)} %got_hbm.1, bf16[400,896]{1,0:T(8,128)(2,1)} %cot_hbm.1), custom_call_target="tpu_custom_call" | custom-call | tf_op jit(solution)/shard_map/gather_rows/pallas_call | solution.py:248
  59.5 0.0 copy-done
  59.5 3.1 %convolution_bitcast_fusion = f32[400,1792]{1,0:T(8,128)S(1)} fusion(bf16[400,2048]{1,0:T(8,128)(2,1)S(1)} %copy-done, bf16[2048,1792]{1,0:T(8,128)(2,1)S(1)} %get-tuple-element.7.weights_ref), kind=kOutput, calls=%fused_computation.1 | convolution fusion | flops 2936012800 | bytes 11845632 | tf_op jit(solution)/shard_map/dot_general | solution.py:575
  62.6 0.7 fusion.4
  63.3 0.1 pad_maximum_fusion.d_ref
  63.5 2.4 %convert_bitcast_fusion.p_ref = bf16[2048,896]{1,0:T(8,128)(2,1)S(1)} fusion(bf16[400,896]{1,0:T(8,128)(2,1)S(1)} %get-tuple-element.11, bf16[400,2048]{1,0:T(8,128)(2,1)S(1)} %copy-done), kind=kOutput, calls=%fused_computation | convolution fusion | flops 1469841408 | bytes 6025216 | tf_op jit(solution)/shard_map/dot_general | solution.py:581
  65.9 44.1 %scatter_sum.1 = (f32[32,896]{1,0:T(8,128)S(1)}, bf16[400,256]{1,0:T(8,128)(2,1)S(1)}) custom-call(bf16[2048,896]{1,0:T(8,128)(2,1)S(1)} %convert_bitcast_fusion.p_ref, bf16[400,1792]{1,0:T(8,128)(2,1)S(1)} %pad_maximum_fusion.d_ref, bf16[2048,1792]{1,0:T(8,128)(2,1)S(1)} %get-tuple-element.7.weights_ref), custom_call_target="tpu_custom_call" | custom-call | tf_op jit(solution)/shard_map/scatter_sum/pallas_call | solution.py:538
  110.0 0.7 copy.12
  110.7 0.6 copy.13
Async XLA Ops:
  0.6 58.9 %copy-start = (bf16[400,2048]{1,0:T(8,128)(2,1)S(1)}, bf16[400,2048]{1,0:T(8,128)(2,1)}, u32[]{:S(2)}) copy-start(bf16[400,2048]{1,0:T(8,128)(2,1)} %param.6) | copy-start | bytes 4915204

commit v6 on v5

--- a/solution.py
+++ b/solution.py
@@ -191,12 +191,11 @@
         y_wait("b", 0, 0, part)
     for way in (0, 1):
         z_copy(2, way, 1).start()
-    a_pass(1, True)
 
     def body(k, carry):
         a_step(k, False)
         b_step(k - 2, False)
-        a_pass(k - 1, False)
+        a_pass(k - 2, False)
         return carry
 
     if top > 4:
@@ -204,9 +203,10 @@
     for k in range(max(3, top - 1), top + 1):
         a_step(k, True)
         b_step(k - 2, True)
-        a_pass(k - 1, True)
+        a_pass(k - 2, True)
+    a_pass(top - 1, True)
+    b_step(top - 1, True)
     a_pass(top, True)
-    b_step(top - 1, True)
     b_step(top, True)
 
     def drain_y(kind, c, zo):
@@ -432,11 +432,13 @@
     b_step(top - 1, True)
     advance()
     ahead(top - 1, True, stage_2)
+    ahead(top - 3, True, stage_1)
 
     def iterate(m, known):
+        if not known or m >= 4:
+            ahead(m - 4, known, stage_1)
         if not known or m >= 3:
             b_step(m - 2, known)
-            ahead(m - 3, known, stage_1)
         if not known or m >= 2:
             ahead(m - 2, known, stage_2)
         a_step(m, known)

time: 111 us -> 111 us (level)
  the two profiles are of different devices: /device:TPU:8 before, /device:TPU:2 now
where the time goes in v6:
time: 111 us
  Pallas kernels  103 us (93%)
  matrix products  5.51 us (5%)
  local copies, waits for them, and re-layouts  1.34 us (1%)
    pallas_call x1, Pallas kernels, gather_rows(): pl.pallas_call(functools.partial(gather_kernel, nz, cut, half_a, half_b),...  61.1 us
    pallas_call x1, Pallas kernels, scatter_sum(): pl.pallas_call(functools.partial(scatter_kernel, nz, peers, cut, half_a,...  41.7 us
    dot_general x1, matrix products, on_device(): both = jnp.dot(x_in, weights, preferred_element_type=jnp.float32)  3.12 us
    dot_general x1, matrix products, on_device(): lax.dot_general(x_in, d_gate, (((0,), (0,)), ((), ())), preferred_element...  2.39 us

profile of v6, /device:TPU:2, one launch (start us, length us, event | category | flops | bytes accessed | tf_op | source)
XLA Modules:
  0.0 111.1 jit_solution(15834791257679230181)
XLA Ops:
  0.6 0.0 copy-start
  0.6 61.1 %gather_rows.1 = (bf16[2048,1792]{1,0:T(8,128)(2,1)S(1)}, bf16[400,896]{1,0:T(8,128)(2,1)S(1)}) custom-call(bf16[32,896]{1,0:T(8,128)(2,1)} %gate_ref.1, bf16[32,896]{1,0:T(8,128)(2,1)} %up_ref.1, s32[1,64]{1,0:T(1,128)} %sent_hbm.1, s32[1,64]{1,0:T(1,128)} %got_hbm.1, bf16[400,896]{1,0:T(8,128)(2,1)} %cot_hbm.1), custom_call_target="tpu_custom_call" | custom-call | tf_op jit(solution)/shard_map/gather_rows/pallas_call | solution.py:248
  61.7 0.0 copy-done
  61.7 3.1 %convolution_bitcast_fusion = f32[400,1792]{1,0:T(8,128)S(1)} fusion(bf16[400,2048]{1,0:T(8,128)(2,1)S(1)} %copy-done, bf16[2048,1792]{1,0:T(8,128)(2,1)S(1)} %get-tuple-element.7.weights_ref), kind=kOutput, calls=%fused_computation.1 | convolution fusion | flops 2936012800 | bytes 11845632 | tf_op jit(solution)/shard_map/dot_general | solution.py:577
  64.9 0.7 fusion.4
  65.6 0.1 pad_maximum_fusion.d_ref
  65.7 2.4 %convert_bitcast_fusion.p_ref = bf16[2048,896]{1,0:T(8,128)(2,1)S(1)} fusion(bf16[400,896]{1,0:T(8,128)(2,1)S(1)} %get-tuple-element.11, bf16[400,2048]{1,0:T(8,128)(2,1)S(1)} %copy-done), kind=kOutput, calls=%fused_computation | convolution fusion | flops 1469841408 | bytes 6025216 | tf_op jit(solution)/shard_map/dot_general | solution.py:583
  68.1 41.7 %scatter_sum.1 = (f32[32,896]{1,0:T(8,128)S(1)}, bf16[400,256]{1,0:T(8,128)(2,1)S(1)}) custom-call(bf16[2048,896]{1,0:T(8,128)(2,1)S(1)} %convert_bitcast_fusion.p_ref, bf16[400,1792]{1,0:T(8,128)(2,1)S(1)} %pad_maximum_fusion.d_ref, bf16[2048,1792]{1,0:T(8,128)(2,1)S(1)} %get-tuple-element.7.weights_ref), custom_call_target="tpu_custom_call" | custom-call | tf_op jit(solution)/shard_map/scatter_sum/pallas_call | solution.py:540
  109.8 0.7 copy.12
  110.4 0.6 copy.13
Async XLA Ops:
  0.6 61.1 %copy-start = (bf16[400,2048]{1,0:T(8,128)(2,1)S(1)}, bf16[400,2048]{1,0:T(8,128)(2,1)}, u32[]{:S(2)}) copy-start(bf16[400,2048]{1,0:T(8,128)(2,1)} %param.6) | copy-start | bytes 4915204

commit v7 on v6

--- a/solution.py
+++ b/solution.py
@@ -437,11 +437,11 @@
     def iterate(m, known):
         if not known or m >= 4:
             ahead(m - 4, known, stage_1)
+        a_step(m, known)
         if not known or m >= 3:
             b_step(m - 2, known)
         if not known or m >= 2:
             ahead(m - 2, known, stage_2)
-        a_step(m, known)
         advance()
 
     for m in range(top, 2, -1):

time: 111 us -> 112 us (level)
  no operation moved by 1% of the time
where the time goes in v7:
time: 112 us
  Pallas kernels  103 us (92%)
  matrix products  5.51 us (5%)
  local copies, waits for them, and re-layouts  1.34 us (1%)
    pallas_call x1, Pallas kernels, gather_rows(): pl.pallas_call(functools.partial(gather_kernel, nz, cut, half_a, half_b),...  61.1 us
    pallas_call x1, Pallas kernels, scatter_sum(): pl.pallas_call(functools.partial(scatter_kernel, nz, peers, cut, half_a,...  42.1 us
    dot_general x1, matrix products, on_device(): both = jnp.dot(x_in, weights, preferred_element_type=jnp.float32)  3.12 us
    dot_general x1, matrix products, on_device(): lax.dot_general(x_in, d_gate, (((0,), (0,)), ((), ())), preferred_element...  2.39 us

profile of v7, /device:TPU:2, one launch (start us, length us, event | category | flops | bytes accessed | tf_op | source)
XLA Modules:
  0.0 111.6 jit_solution(9659490954715712204)
XLA Ops:
  0.6 0.0 copy-start
  0.6 61.1 %gather_rows.1 = (bf16[2048,1792]{1,0:T(8,128)(2,1)S(1)}, bf16[400,896]{1,0:T(8,128)(2,1)S(1)}) custom-call(bf16[32,896]{1,0:T(8,128)(2,1)} %gate_ref.1, bf16[32,896]{1,0:T(8,128)(2,1)} %up_ref.1, s32[1,64]{1,0:T(1,128)} %sent_hbm.1, s32[1,64]{1,0:T(1,128)} %got_hbm.1, bf16[400,896]{1,0:T(8,128)(2,1)} %cot_hbm.1), custom_call_target="tpu_custom_call" | custom-call | tf_op jit(solution)/shard_map/gather_rows/pallas_call | solution.py:248
  61.7 0.0 copy-done
  61.7 3.1 %convolution_bitcast_fusion = f32[400,1792]{1,0:T(8,128)S(1)} fusion(bf16[400,2048]{1,0:T(8,128)(2,1)S(1)} %copy-done, bf16[2048,1792]{1,0:T(8,128)(2,1)S(1)} %get-tuple-element.7.weights_ref), kind=kOutput, calls=%fused_computation.1 | convolution fusion | flops 2936012800 | bytes 11845632 | tf_op jit(solution)/shard_map/dot_general | solution.py:577
  64.9 0.7 fusion.4
  65.6 0.1 pad_maximum_fusion.d_ref
  65.7 2.4 %convert_bitcast_fusion.p_ref = bf16[2048,896]{1,0:T(8,128)(2,1)S(1)} fusion(bf16[400,896]{1,0:T(8,128)(2,1)S(1)} %get-tuple-element.11, bf16[400,2048]{1,0:T(8,128)(2,1)S(1)} %copy-done), kind=kOutput, calls=%fused_computation | convolution fusion | flops 1469841408 | bytes 6025216 | tf_op jit(solution)/shard_map/dot_general | solution.py:583
  68.1 42.1 %scatter_sum.1 = (f32[32,896]{1,0:T(8,128)S(1)}, bf16[400,256]{1,0:T(8,128)(2,1)S(1)}) custom-call(bf16[2048,896]{1,0:T(8,128)(2,1)S(1)} %convert_bitcast_fusion.p_ref, bf16[400,1792]{1,0:T(8,128)(2,1)S(1)} %pad_maximum_fusion.d_ref, bf16[2048,1792]{1,0:T(8,128)(2,1)S(1)} %get-tuple-element.7.weights_ref), custom_call_target="tpu_custom_call" | custom-call | tf_op jit(solution)/shard_map/scatter_sum/pallas_call | solution.py:540
  110.2 0.7 copy.12
  110.9 0.6 copy.13
Async XLA Ops:
  0.6 61.1 %copy-start = (bf16[400,2048]{1,0:T(8,128)(2,1)S(1)}, bf16[400,2048]{1,0:T(8,128)(2,1)}, u32[]{:S(2)}) copy-start(bf16[400,2048]{1,0:T(8,128)(2,1)} %param.6) | copy-start | bytes 4915204
